TPU v7x, 32 devices: a whole 2x2x4 slice. The times are simulated.
32 devices in a mesh: node: 4 (over y, core), cores: 8 (over z, x).
Axes of the slice: x: 2, y: 2, z: 4, core: 2. Of those that a mesh axis runs over, the one named last changes fastest.
Arguments:
- fitted: bfloat16 [16, 256, 256, 256], P(None, ('node', 'cores')), may hold values from -0.09375 to 0.09375
- fit_mask: int32 [16, 32], replicated, may hold values 0 or 1
- tasks: int32 [16, 2], replicated, may hold values from 0 to 15, as said below
- owner_map: int32 [16], replicated, may hold values from 0 to 15, each once
- partner: int32 [4], replicated, may hold values from 0 to 3, as said below
- amplitudes: float32 [16, 4, 256, 256], P('cores', None, 'node'), may hold values from -6 to 6
- pair_energy: float32 [4], replicated, may hold values from -1.2 to -0.6
- virt_energy: float32 [1024], replicated, may hold values from 0.1 to 1.2
Outputs:
- new_amplitudes: float32 [16, 4, 256, 256], P('cores', None, 'node')
Inputs may be any that keep to these rules, and one draw needn't show every extreme that they name: `tasks`: each row names an output tile pair and an input tile pair, both numbered X * 4 + Y; no two rows are equal. `owner_map`: each tile pair appears once. partner[partner[p]] = p and partner[p] != p.
All inputs are finite; a program needn't handle non-finite values.
Results may differ from a plain program's by a relative error of at most 0.00057.
Values may be sent and summed in bfloat16 or wider, within the bound.
No kernel may reach another device: no remote copies, remote signals or barrier semaphores. Data moves between devices by JAX's collectives and lax.ppermute only.
A program may use at most 192 MiB of HBM per device.

v0:
```python
import math

import jax
import jax.numpy as jnp
from jax import lax
from jax.sharding import PartitionSpec as P


def slot_lookup(owner_map):
    count_all = owner_map.shape[0]
    places = jnp.arange(count_all, dtype=jnp.int32)
    hits = owner_map[None, :] == places[:, None]
    return jnp.sum(jnp.where(hits, places[None, :], 0), axis=1)


def body(fitted, fit_mask, tasks, owner_map, partner, amplitudes, pair_energy, virt_energy):
    pair_count = amplitudes.shape[1]
    tile_width = amplitudes.shape[3]
    rows_here = amplitudes.shape[2]
    slot_count = amplitudes.shape[0]
    tile_pairs = owner_map.shape[0]
    side_count = math.isqrt(tile_pairs)
    block_index = lax.axis_index(("node", "cores"))
    core_index = lax.axis_index("cores")
    node_index = lax.axis_index("node")
    lowered = amplitudes.astype(jnp.bfloat16)
    rows_whole = lax.all_gather(lowered, "node", axis=2, tiled=True)
    every_slot = lax.all_gather(rows_whole, "cores", axis=0, tiled=True)
    slot_of = slot_lookup(owner_map)
    mask_column = lax.dynamic_slice_in_dim(fit_mask, block_index, 1, 1)[:, 0]

    def task_step(task_number, running):
        out_tile = tasks[task_number, 0]
        in_tile = tasks[task_number, 1]
        left_index = out_tile // side_count * side_count + in_tile // side_count
        right_index = out_tile % side_count * side_count + in_tile % side_count
        active = mask_column[left_index] * mask_column[right_index]

        def compute(unused):
            left_factor = fitted[left_index]
            right_factor = fitted[right_index]
            amplitude_tile = every_slot[slot_of[in_tile]]
            half_product = jnp.einsum(
                "qac,pcd->qpad", left_factor, amplitude_tile, preferred_element_type=jnp.float32
            ).astype(jnp.bfloat16)
            return jnp.einsum(
                "qpad,qbd->pab", half_product, right_factor, preferred_element_type=jnp.float32
            )

        def nothing(unused):
            return jnp.zeros((pair_count, tile_width, tile_width), jnp.float32)

        contrib = lax.cond(active > 0, compute, nothing, 0)
        return running.at[out_tile].add(contrib)

    ladder_sum = lax.fori_loop(
        0,
        tasks.shape[0],
        task_step,
        jnp.zeros((tile_pairs, pair_count, tile_width, tile_width), jnp.float32),
    )
    grid = ladder_sum.reshape(side_count, side_count, pair_count, tile_width, tile_width)
    flipped = jnp.transpose(grid, (1, 0, 2, 4, 3)).reshape(ladder_sum.shape)
    flipped = jnp.take(flipped, partner, axis=1)
    summed_term = 0.5 * (ladder_sum + flipped)
    slot_term = jnp.take(summed_term, owner_map, axis=0)
    own_rows = lax.psum_scatter(slot_term, "node", scatter_dimension=2, tiled=True)
    symmetric = lax.psum_scatter(own_rows, "cores", scatter_dimension=0, tiled=True)
    my_tiles = lax.dynamic_slice_in_dim(owner_map, core_index * slot_count, slot_count)
    row_tiles = my_tiles // side_count
    col_tiles = my_tiles % side_count

    def energy_rows(tile_number):
        return lax.dynamic_slice_in_dim(
            virt_energy, tile_number * tile_width + node_index * rows_here, rows_here
        )

    def energy_cols(tile_number):
        return lax.dynamic_slice_in_dim(virt_energy, tile_number * tile_width, tile_width)

    row_energy = jax.vmap(energy_rows)(row_tiles)
    col_energy = jax.vmap(energy_cols)(col_tiles)
    denominator = (
        pair_energy[None, :, None, None]
        - row_energy[:, None, :, None]
        - col_energy[:, None, None, :]
    )
    return amplitudes + symmetric / denominator


def solution(mesh):
    placed = (
        P(None, ("node", "cores"), None, None),
        P(),
        P(),
        P(),
        P(),
        P("cores", None, "node", None),
        P(),
        P(),
    )
    return jax.shard_map(
        body, mesh=mesh, in_specs=placed, out_specs=P("cores", None, "node", None), check_vma=False
    )
```

profile of v0, /device:TPU:0, one launch (start us, length us, event | category | flops | bytes accessed | tf_op | source)
XLA Modules:
  0.0 809.4 jit_solution(3937791093901708205)
XLA Ops:
  8.7 19.7 %all-gather.3.cloned.1.call-done = bf16[2,4,256,256]{3,1,0,2:T(4,128)(2,1)} async-done(((bf16[2,4,64,256]{3,1,0,2:T(4,128)(2,1)}), bf16[2,4,256,256]{3,1,0,2:T(4,128)(2,1)}) %all-gather.3.cloned.1.call-update) | async-done | bytes 1048592 | tf_op jit(solution)/shard_map/all_gather | solution.py:27
  34.5 121.4 %all-gather.5.cloned.1.call-done = bf16[16,4,256,256]{3,2,1,0:T(8,128)(2,1)} async-done(((bf16[2,4,256,256]{3,2,1,0:T(8,128)(2,1)}), bf16[16,4,256,256]{3,2,1,0:T(8,128)(2,1)}) %all-gather.5.cloned.1.call-update) | async-done | bytes 8388624 | tf_op jit(solution)/shard_map/all_gather | solution.py:28
  155.9 12.3 %copy.26 = bf16[16,4,256,256]{2,3,1,0:T(8,128)(2,1)} copy(bf16[16,4,256,256]{3,2,1,0:T(8,128)(2,1)} %all-gather.5.cloned.1.call-done) | data formatting | bytes 16777216 | tf_op jit(solution)/shard_map/while | solution.py:56
  168.1 7.8 broadcast_in_dim.53
  175.9 247.3 %while.19 = (s32[]{:T(128)}, f32[16,4,256,256]{3,2,1,0:T(8,128)}, s32[16,2]{0,1:T(2,128)S(1)}, s32[16]{0:T(128)S(1)}, s32[16]{0:T(128)S(1)}, /*index=5*/bf16[16,...) while((s32[]{:T(128)}, f32[16,4,256,256]{3,2,1,0:T(8,128)}, ...), condition=%wide.region_5.6_spmd, body=%wide.region_1.5_spmd.sunk | while | flops 2150105088 | bytes 6817743 | solution.py:56
  234.9 3.2 fusion.31
  245.3 8.2 %conditional.2 = (f32[1,4,256,256]{3,2,1,0:T(8,128)S(1)}) conditional(s32[]{:T(128)} %bitcast.55, () %tuple.87, (s32[]{:T(128)}, s32[16]{0:T(128)S(1)}, bf16[16,4,256,256]{2,3,1,0:T(8,128)(2,1)}, s32[]{:T(128)}, bf16[16,8,256,256]{3,2,1,0:T(8,128)(2,1)}, /*index=5*/s32[]{:T(128)}) %tuple.88), branch_computations={%region_3.3_spmd, %region_4.4_spmd} | conditional | flops 2149580800 | bytes 3670184 | solution.py:53
  249.2 4.3 fusion.5
  255.5 3.2 fusion.31
  278.3 8.2 %conditional.2 = (f32[1,4,256,256]{3,2,1,0:T(8,128)S(1)}) conditional(s32[]{:T(128)} %bitcast.55, () %tuple.87, (s32[]{:T(128)}, s32[16]{0:T(128)S(1)}, bf16[16,4,256,256]{2,3,1,0:T(8,128)(2,1)}, s32[]{:T(128)}, bf16[16,8,256,256]{3,2,1,0:T(8,128)(2,1)}, /*index=5*/s32[]{:T(128)}) %tuple.88), branch_computations={%region_3.3_spmd, %region_4.4_spmd} | conditional | flops 2149580800 | bytes 3670184 | solution.py:53
  282.2 4.3 fusion.5
  311.2 8.2 %conditional.2 = (f32[1,4,256,256]{3,2,1,0:T(8,128)S(1)}) conditional(s32[]{:T(128)} %bitcast.55, () %tuple.87, (s32[]{:T(128)}, s32[16]{0:T(128)S(1)}, bf16[16,4,256,256]{2,3,1,0:T(8,128)(2,1)}, s32[]{:T(128)}, bf16[16,8,256,256]{3,2,1,0:T(8,128)(2,1)}, /*index=5*/s32[]{:T(128)}) %tuple.88), branch_computations={%region_3.3_spmd, %region_4.4_spmd} | conditional | flops 2149580800 | bytes 3670184 | solution.py:53
  315.1 4.3 fusion.5
  331.7 8.2 %conditional.2 = (f32[1,4,256,256]{3,2,1,0:T(8,128)S(1)}) conditional(s32[]{:T(128)} %bitcast.55, () %tuple.87, (s32[]{:T(128)}, s32[16]{0:T(128)S(1)}, bf16[16,4,256,256]{2,3,1,0:T(8,128)(2,1)}, s32[]{:T(128)}, bf16[16,8,256,256]{3,2,1,0:T(8,128)(2,1)}, /*index=5*/s32[]{:T(128)}) %tuple.88), branch_computations={%region_3.3_spmd, %region_4.4_spmd} | conditional | flops 2149580800 | bytes 3670184 | solution.py:53
  335.6 4.3 fusion.5
  366.7 3.1 fusion.31
  389.4 8.2 %conditional.2 = (f32[1,4,256,256]{3,2,1,0:T(8,128)S(1)}) conditional(s32[]{:T(128)} %bitcast.55, () %tuple.87, (s32[]{:T(128)}, s32[16]{0:T(128)S(1)}, bf16[16,4,256,256]{2,3,1,0:T(8,128)(2,1)}, s32[]{:T(128)}, bf16[16,8,256,256]{3,2,1,0:T(8,128)(2,1)}, /*index=5*/s32[]{:T(128)}) %tuple.88), branch_computations={%region_3.3_spmd, %region_4.4_spmd} | conditional | flops 2149580800 | bytes 3670184 | solution.py:53
  393.3 4.3 fusion.5
  409.9 8.2 %conditional.2 = (f32[1,4,256,256]{3,2,1,0:T(8,128)S(1)}) conditional(s32[]{:T(128)} %bitcast.55, () %tuple.87, (s32[]{:T(128)}, s32[16]{0:T(128)S(1)}, bf16[16,4,256,256]{2,3,1,0:T(8,128)(2,1)}, s32[]{:T(128)}, bf16[16,8,256,256]{3,2,1,0:T(8,128)(2,1)}, /*index=5*/s32[]{:T(128)}) %tuple.88), branch_computations={%region_3.3_spmd, %region_4.4_spmd} | conditional | flops 2149580800 | bytes 3670184 | solution.py:53
  413.8 4.3 fusion.5
  420.1 3.1 fusion.31
  423.2 19.2 %copy.27 = f32[4,4,4,256,256]{4,3,2,1,0:T(8,128)} copy(f32[4,4,4,256,256]{3,4,2,0,1:T(8,128)} %bitcast.61) | data formatting | bytes 33554432 | tf_op jit(solution)/shard_map/transpose | solution.py:63
  442.4 11.0 %fusion.27 = (f32[16,4,128,256]{3,2,1,0:T(8,128)}, f32[16,4,128,256]{3,2,1,0:T(8,128)}) fusion(f32[16,4,256,256]{3,2,1,0:T(8,128)} %bitcast.62), kind=kLoop, calls=%fused_computation.50 | loop fusion | bytes 33554432 | tf_op jit(solution)/shard_map/jit(_take)/gather | solution.py:64
  453.4 7.7 gather_fusion.1
  461.1 7.7 gather_fusion.2
  468.7 17.7 %fusion.22 = f32[16,4,256,256]{3,2,0,1:T(8,128)} fusion(f32[16,4,128,256]{3,2,0,1:T(8,128)} %bitcast.64, f32[16,4,128,256]{3,2,0,1:T(8,128)} %bitcast.63, f32[16,4,256,256]{3,2,1,0:T(8,128)} %get-tuple-element.262, pred[4]{0:T(512)(128)(4,1)S(1)} %compare_and_fusion), kind=kLoop, calls=%fused_computation.25 | loop fusion | flops 16777216 | bytes 50331652 | tf_op jit(solution)/shard_map/mul | solution.py:65
  486.4 13.9 %gather_fusion = f32[16,4,256,256]{3,2,1,0:T(8,128)} fusion(f32[16,4,256,256]{3,2,0,1:T(8,128)} %fusion.22, s32[1024]{0:T(1024)S(1)} %pad_clamp_fusion), kind=kCustom, calls=%fused_computation | custom fusion | bytes 33554496 | tf_op jit(solution)/shard_map/jit(_take)/gather | solution.py:66
  500.3 11.6 %broadcast_select_fusion = f32[16,4,256,256]{3,2,1,0:T(8,128)} fusion(f32[16,4,256,256]{3,2,1,0:T(8,128)} %gather_fusion, pred[16]{0:T(512)(128)(4,1)S(1)} %compare_and_fusion.1), kind=kLoop, calls=%fused_computation.26 | loop fusion | flops 4194304 | bytes 33554448 | tf_op jit(solution)/shard_map/jit(_take)/select_n | solution.py:66
  512.0 197.0 %reduce-scatter.3.cloned.1.call-done = f32[16,4,64,256]{3,2,1,0:T(8,128)} async-done(((f32[16,4,256,256]{3,2,1,0:T(8,128)}), f32[16,4,64,256]{3,2,1,0:T(8,128)}) %reduce-scatter.3.cloned.1.call-update) | async-done | bytes 4194320 | tf_op jit(solution)/shard_map/reduce_scatter | solution.py:67
  709.2 4.2 while.21
  713.3 4.1 while.20
  717.5 83.4 %reduce-scatter.5.cloned.1.call-done = f32[2,4,64,256]{3,2,1,0:T(8,128)} async-done(((f32[16,4,64,256]{3,2,1,0:T(8,128)}), f32[2,4,64,256]{3,2,1,0:T(8,128)}) %reduce-scatter.5.cloned.1.call-update) | async-done | bytes 524304 | tf_op jit(solution)/shard_map/reduce_scatter | solution.py:68
  (136 shorter events, 93.1 us)
Async XLA Ops:
  6.5 24.3 %copy-start = (s32[16,32]{1,0:T(8,128)S(1)}, s32[16,32]{1,0:T(8,128)}, u32[]{:S(2)}) copy-start(s32[16,32]{1,0:T(8,128)} %param.15) | copy-start | bytes 6148
  6.5 21.8 %all-gather.3.cloned.1.call-start = ((), (), s32[]{:S(2)}) async-start(), calls=%async_computation.2 | async-start | bytes 1310720 | tf_op jit(solution)/shard_map/all_gather | solution.py:27
  8.7 147.2 %all-gather.5.cloned.1.call-start = ((), (), s32[]{:S(2)}) async-start(), calls=%async_computation.3 | async-start | bytes 9437184 | tf_op jit(solution)/shard_map/all_gather | solution.py:28
  30.8 678.2 %reduce-scatter.3.cloned.1.call-start = ((), (), s32[]{:S(2)}) async-start(), calls=%async_computation.4 | async-start | bytes 20971520 | tf_op jit(solution)/shard_map/reduce_scatter | solution.py:67
  34.5 141.4 %copy-start.3 = (s32[16,2]{0,1:T(2,128)S(1)}, s32[16,2]{0,1:T(2,128)}, u32[]{:S(2)}) copy-start(s32[16,2]{0,1:T(2,128)} %param.16) | copy-start | bytes 388
  34.5 141.4 %copy-start.4 = (s32[4]{0:T(128)S(1)}, s32[4]{0:T(128)}, u32[]{:S(2)}) copy-start(s32[4]{0:T(128)} %constant.239.clone.1) | copy-start | bytes 52
  500.3 302.6 %copy-start.1 = (s32[16,32]{1,0:T(8,128)S(1)}, s32[16,32]{1,0:T(8,128)}, u32[]{:S(2)}) copy-start(s32[16,32]{1,0:T(8,128)} %param.15) | copy-start | bytes 6148
  511.9 197.1 %copy-start.5 = (s32[16]{0:T(128)S(1)}, s32[16]{0:T(128)}, u32[]{:S(2)}) copy-start(s32[16]{0:T(128)} %param.17) | copy-start | bytes 196
  511.9 205.5 %copy-start.6 = (f32[4]{0:T(128)S(1)}, f32[4]{0:T(128)}, u32[]{:S(2)}) copy-start(f32[4]{0:T(128)} %param.20) | copy-start | bytes 52
  511.9 289.0 %copy-start.2 = (f32[2,4,64,256]{3,2,1,0:T(8,128)S(1)}, f32[2,4,64,256]{3,2,1,0:T(8,128)}, u32[]{:S(2)}) copy-start(f32[2,4,64,256]{3,2,1,0:T(8,128)} %param.19) | copy-start | bytes 1572868
  512.0 288.9 %reduce-scatter.5.cloned.1.call-start = ((), (), s32[]{:S(2)}) async-start(), calls=%async_computation.5 | async-start | bytes 4718592 | tf_op jit(solution)/shard_map/reduce_scatter | solution.py:68
Sparse Core Ops, SparseCore 0:
  8.9 19.4 all-gather.2
  30.9 124.9 all-gather.4
  512.1 196.8 reduce-scatter.2
  712.9 87.9 reduce-scatter.4
where the time goes:
time: 819 us; the launch traced here: 809 us
  waiting for transfers between devices  422 us (52%)
  loops' own time  136 us (17%)
  local copies, waits for them, and re-layouts  116 us (14%)
  other arithmetic  96.9 us (12%)
  matrix products  25.7 us (3%)
  between operations  13.2 us (2%)
    reduce_scatter x1, waiting for transfers between devices, body(): lax.psum_scatter(slot_term, 'node', scatter_dimension=2, tiled=True)  197 us
    all_gather x1, waiting for transfers between devices, body(): every_slot = lax.all_gather(rows_whole, 'cores', axis=0, tiled=True)  121 us
    another operation x1, loops' own time, body(): lax.fori_loop(0, tasks.shape[0], task_step, jnp.zeros((tile_pairs, pair_c...  115 us
    reduce_scatter x1, waiting for transfers between devices, body(): lax.psum_scatter(own_rows, 'cores', scatter_dimension=0, tiled=True)  83.4 us
    scatter-add x16, other arithmetic, task_step(): return running.at[out_tile].add(contrib)  49.6 us
    gather x3, local copies, waits for them, and re-layouts, body(): flipped = jnp.take(flipped, partner, axis=1)  26.3 us
    dot_general x6, matrix products, compute(): jnp.einsum('qpad,qbd->pab', half_product, right_factor, preferred_element...  25.7 us
    another operation x16, loops' own time, task_step(): contrib = lax.cond(active > 0, compute, nothing, 0)  20.3 us
  transfers between devices with their start and end apart: 4, of which 4 were waited for; matrix products, arithmetic and copies ran while one was open for 1% of the time, Pallas kernels for 0%

commit v1 on v0

v1 whole, which is shorter than its diff:
```python
import functools
import math

import jax
import jax.numpy as jnp
from jax import lax
from jax.experimental import pallas as pl
from jax.experimental.pallas import tpu as pltpu
from jax.sharding import PartitionSpec as P

AXES = ("node", "cores")


def ladder_kernel(
    dims, mask_ref, tasks_ref, owner_ref, partner_ref, fitted_ref, amps_ref, keep_ref, send_ref,
    left_buf, right_buf, tile_buf, total, work, slot_of, rank_of, load_sems, store_sems,
):
    nodes, cores, slots_here, pairs, rows, tile, aux, slots, side = dims
    task_count = tasks_ref.shape[0]
    node_index = lax.axis_index("node")
    core_index = lax.axis_index("cores")
    block = node_index * cores + core_index

    def invert(s, carry):
        slot_of[owner_ref[s]] = s
        return carry

    lax.fori_loop(0, slots, invert, 0)

    def rank(p, count):
        is_rep = p < partner_ref[p]

        @pl.when(is_rep)
        def _():
            rank_of[p] = count
            rank_of[partner_ref[p]] = count

        return count + is_rep.astype(jnp.int32)

    lax.fori_loop(0, pairs, rank, jnp.int32(0))

    def indices(t):
        out_tile = tasks_ref[t, 0]
        in_tile = tasks_ref[t, 1]
        a, b = out_tile // side, out_tile % side
        c, d = in_tile // side, in_tile % side
        return a, b, a * side + c, b * side + d, in_tile

    def enlist(t, count):
        _, _, left, right, _ = indices(t)
        work[count] = t
        return count + mask_ref[left, block] * mask_ref[right, block]

    active = lax.fori_loop(0, task_count, enlist, jnp.int32(0))

    def loads(i, slot):
        _, _, left, right, in_tile = indices(work[i])
        place = slot_of[in_tile]
        owner = place // slots_here
        inside = place % slots_here
        copies = [pltpu.make_async_copy(fitted_ref.at[left], left_buf.at[slot], load_sems.at[slot, 0])]
        for q in range(aux):
            copies.append(
                pltpu.make_async_copy(
                    fitted_ref.at[right, q], right_buf.at[slot, pairs, :, pl.ds(q * tile, tile)], load_sems.at[slot, 1]
                )
            )
        for n in range(nodes):
            copies.append(
                pltpu.make_async_copy(
                    amps_ref.at[n * cores + owner, inside],
                    tile_buf.at[slot, :, pl.ds(n * rows, rows), :],
                    load_sems.at[slot, 2],
                )
            )
        return copies

    @pl.when(active > 0)
    def _():
        for copy in loads(0, 0):
            copy.start()

    @pl.loop(0, slots)
    def _(s):
        total[s] = jnp.zeros(total.shape[1:], jnp.float32)

    @pl.loop(0, active)
    def _(i):
        slot = i % 2

        @pl.when(i + 1 < active)
        def _():
            for copy in loads(i + 1, 1 - slot):
                copy.start()

        for copy in loads(i, slot):
            copy.wait()
        a, b, _, _, _ = indices(work[i])
        straight = slot_of[a * side + b]
        crossed = slot_of[b * side + a]
        left_all = left_buf[slot].reshape(aux * tile, tile)
        for p in range(pairs):
            half = jnp.dot(left_all, tile_buf[slot, p], preferred_element_type=jnp.float32).astype(jnp.bfloat16)
            for q in range(aux):
                right_buf[slot, p, :, q * tile:(q + 1) * tile] = half[q * tile:(q + 1) * tile]
        for p in range(pairs):
            is_rep = p < partner_ref[p]
            first = jnp.where(is_rep, p, pairs)
            second = jnp.where(is_rep, pairs, p)
            place = jnp.where(is_rep, straight, crossed)
            which = rank_of[p]
            total[place, which] += lax.dot_general(
                right_buf[slot, first], right_buf[slot, second], (((1,), (1,)), ((), ())),
                preferred_element_type=jnp.float32,
            )

    mine = node_index % 2
    stores = [
        pltpu.make_async_copy(total.at[:, mine], keep_ref, store_sems.at[0]),
        pltpu.make_async_copy(total.at[:, 1 - mine], send_ref, store_sems.at[1]),
    ]
    for copy in stores:
        copy.start()
    for copy in stores:
        copy.wait()


def ladder_terms(mask, tasks, owner_map, partner, fitted, gathered, nodes, cores):
    tile_pairs, aux, tile, _ = fitted.shape
    slots_here, pairs, rows = gathered.shape[1:4]
    side = math.isqrt(tile_pairs)
    dims = (nodes, cores, slots_here, pairs, rows, tile, aux, tile_pairs, side)
    smem = pl.BlockSpec(memory_space=pltpu.SMEM)
    hbm = pl.BlockSpec(memory_space=pl.ANY)
    part = jax.ShapeDtypeStruct((tile_pairs, tile, tile), jnp.float32)
    return pl.pallas_call(
        functools.partial(ladder_kernel, dims),
        out_shape=(part, part),
        in_specs=[smem, smem, smem, smem, hbm, hbm],
        out_specs=(hbm, hbm),
        scratch_shapes=[
            pltpu.VMEM((2, aux, tile, tile), jnp.bfloat16),
            pltpu.VMEM((2, pairs + 1, tile, aux * tile), jnp.bfloat16),
            pltpu.VMEM((2, pairs, tile, tile), jnp.bfloat16),
            pltpu.VMEM((tile_pairs, pairs // 2, tile, tile), jnp.float32),
            pltpu.SMEM((tasks.shape[0] + 1,), jnp.int32),
            pltpu.SMEM((tile_pairs,), jnp.int32),
            pltpu.SMEM((pairs,), jnp.int32),
            pltpu.SemaphoreType.DMA((2, 3)),
            pltpu.SemaphoreType.DMA((2,)),
        ],
        compiler_params=pltpu.CompilerParams(vmem_limit_bytes=48 * 1024 * 1024),
        cost_estimate=pl.CostEstimate(flops=40 * 10**9, bytes_accessed=48 * 2**20, transcendentals=0),
        name="ladder",
    )(mask, tasks, owner_map, partner, fitted, gathered)


def swap(array, mask, total):
    return lax.ppermute(array, AXES, [(i, i ^ mask) for i in range(total)])


def pick(array, index, axis):
    return lax.dynamic_index_in_dim(array, index, axis, keepdims=False)


def body(nodes, cores, fitted, fit_mask, tasks, owner_map, partner, amplitudes, pair_energy, virt_energy):
    slots_here, pairs, rows, tile = amplitudes.shape
    tile_pairs = owner_map.shape[0]
    side = math.isqrt(tile_pairs)
    total = nodes * cores
    node_index = lax.axis_index("node")
    core_index = lax.axis_index("cores")
    f32, f16 = jnp.float32, jnp.float16
    scale = 2.0 ** -9

    lowered = amplitudes.astype(jnp.bfloat16)
    gathered = lax.all_gather(lowered, AXES, axis=0, tiled=False)
    keep, send = ladder_terms(fit_mask, tasks, owner_map, partner, fitted, gathered, nodes, cores)

    got = swap(send, cores, total)
    inner = nodes // 2
    cuts = inner // slots_here
    strip = rows // cuts
    part = (keep + got) * scale
    part = part.reshape(cores, slots_here, nodes, cuts, strip, tile).transpose(0, 1, 3, 2, 4, 5)
    part = part.reshape(cores, inner, nodes * strip, tile).astype(f16)

    def halve(value, index, axis_size, axis, mask):
        shape = value.shape
        inner_shape = (axis_size // 2, 2)
        split = value.reshape(shape[:axis] + inner_shape + shape[axis + 1:])
        other = swap(pick(split, 1 - index, axis + 1), mask, total)
        own = pick(split, index, axis + 1)
        return (own.astype(f32) + other.astype(f32)).astype(f16)

    def over_inner(value):
        mask, index = 2 * cores, node_index // 2
        while value.shape[1] > 1:
            value = halve(value, index % 2, value.shape[1], 1, mask)
            mask, index = mask * 2, index // 2
        return value[:, 0]

    def over_low(value):
        return halve(value, core_index % 2, value.shape[0], 0, 1)

    half_rows = part.shape[2] // 2
    upper = over_low(over_inner(part[:, :, :half_rows]))
    lower = over_inner(over_low(part[:, :, half_rows:]))
    part = jnp.concatenate([upper, lower], axis=1)
    far = part.shape[0]
    at = core_index // 2
    mine = pick(part, at, 0).astype(f32)
    for step in range(1, far):
        mine = mine + swap(pick(part, at ^ step, 0), 2 * step, total).astype(f32)

    mine = mine * (0.5 / scale)
    blocks_here = slots_here * 2
    straight = mine.reshape(nodes, strip, tile)
    turned = mine.reshape(nodes, strip, nodes, rows).transpose(2, 3, 0, 1)
    if cuts == 1:
        both = jnp.stack([straight, turned.reshape(nodes, rows, tile)], axis=1)
        every = lax.all_to_all(both, "node", 0, 0, tiled=True)
        own_rows = every[:, 0]
        own_cols = every[:, 1]
    else:
        own_rows = lax.all_to_all(straight, "node", 0, 0, tiled=True)
        own_rows = own_rows.reshape(slots_here, cuts, 2, strip, tile).transpose(0, 2, 1, 3, 4)
        own_cols = lax.all_to_all(turned, "node", 0, 0, tiled=True)
        own_cols = own_cols.reshape(slots_here, cuts, 2, rows, nodes, strip).transpose(0, 2, 3, 4, 1, 5)
    own_rows = own_rows.reshape(slots_here, 2, rows, tile)
    own_cols = own_cols.reshape(slots_here, 2, rows, tile)
    all_cols = lax.all_gather(own_cols, "cores", axis=0, tiled=True)

    places = jnp.arange(tile_pairs, dtype=jnp.int32)
    slot_of = jnp.sum(jnp.where(owner_map[None, :] == places[:, None], places[None, :], 0), axis=1)
    my_tiles = lax.dynamic_slice_in_dim(owner_map, core_index * slots_here, slots_here)
    row_tiles, col_tiles = my_tiles // side, my_tiles % side
    pair_ids = jnp.arange(pairs, dtype=jnp.int32)
    is_rep = pair_ids < partner
    low = jnp.minimum(pair_ids, partner)
    ranks = jnp.sum((is_rep[None, :] & (pair_ids[None, :] < low[:, None])).astype(jnp.int32), axis=1)
    out = []
    for j in range(slots_here):
        crossed = pick(all_cols, slot_of[col_tiles[j] * side + row_tiles[j]], 0)
        symmetric = jnp.stack(
            [jnp.where(is_rep[p], pick(own_rows[j], ranks[p], 0), pick(crossed, ranks[p], 0)) for p in range(pairs)]
        )
        row_energy = lax.dynamic_slice_in_dim(virt_energy, row_tiles[j] * tile + node_index * rows, rows)
        col_energy = lax.dynamic_slice_in_dim(virt_energy, col_tiles[j] * tile, tile)
        denominator = (pair_energy[:, None, None] - row_energy[None, :, None]) - col_energy[None, None, :]
        out.append(amplitudes[j] + symmetric / denominator)
    return jnp.stack(out)


def solution(mesh):
    placed = (P(None, AXES, None, None), P(), P(), P(), P(), P("cores", None, "node", None), P(), P())
    return jax.shard_map(
        functools.partial(body, mesh.shape["node"], mesh.shape["cores"]),
        mesh=mesh, in_specs=placed, out_specs=P("cores", None, "node", None), check_vma=False,
    )
```

time: 819 us -> 256 us (0.31)
  waiting for transfers between devices: 422 us -> 143 us
  loops' own time: 136 us -> 0 us
  local copies, waits for them, and re-layouts: 116 us -> 13.2 us
  other arithmetic: 96.9 us -> 12.3 us
  Pallas kernels: 0 us -> 26.3 us
  matrix products: 25.7 us -> 0 us
  starting transfers between devices: 0.13 us -> 17.5 us
  between operations: 13.2 us -> 30.4 us
  blocking collectives: 0 us -> 11.2 us
    reduce_scatter x2 -> x0, waiting for transfers between devices: 280 us -> none  [the longest x1 197 us: body(): lax.psum_scatter(slot_term, 'node', scatter_dimension=2, tiled=True)]
    another operation x19 -> x0, loops' own time: 136 us -> none  [the longest x1 115 us: body(): lax.fori_loop(0, tasks.shape[0], task_step, jnp.zeros((tile_pairs, pair_c...]
    scatter-add x16 -> x0, other arithmetic: 49.6 us -> none  [task_step(): return running.at[out_tile].add(contrib)]
    gather x16 -> x0, local copies, waits for them, and re-layouts: 48.4 us -> none  [the longest x3 26.3 us: body(): flipped = jnp.take(flipped, partner, axis=1)]
    ppermute x0 -> x8, waiting for transfers between devices: none -> 35.5 us  [swap(): return lax.ppermute(array, AXES, [(i, i ^ mask) for i in range(total)])]
    all_gather x2, waiting for transfers between devices: 141 us -> 107 us  [the longest x1 81.3 us: body(): gathered = lax.all_gather(lowered, AXES, axis=0, tiled=False)]
    pallas_call x0 -> x1, Pallas kernels: none -> 26.3 us  [ladder_terms(): pl.pallas_call(functools.partial(ladder_kernel, dims), out_shape=(part, p...]
    dot_general x6 -> x0, matrix products: 25.7 us -> none  [compute(): jnp.einsum('qpad,qbd->pab', half_product, right_factor, preferred_element...]
  transfers between devices with their start and end apart: 4 -> 10, of which waited for: 4 -> 9; matrix products, arithmetic and copies ran while one was open for 1% -> 3% of each run, Pallas kernels for 0% -> 0%
where the time goes in v1:
time: 256 us; the launch traced here: 254 us
  waiting for transfers between devices  143 us (56%)
  between operations  30.4 us (12%)
  Pallas kernels  26.3 us (10%)
  starting transfers between devices  17.5 us (7%)
  local copies, waits for them, and re-layouts  13.2 us (5%)
  other arithmetic  12.3 us (5%)
  blocking collectives  11.2 us (4%)
    all_gather x1, waiting for transfers between devices, body(): gathered = lax.all_gather(lowered, AXES, axis=0, tiled=False)  81.3 us
    ppermute x8, waiting for transfers between devices, swap(): return lax.ppermute(array, AXES, [(i, i ^ mask) for i in range(total)])  35.5 us
    pallas_call x1, Pallas kernels, ladder_terms(): pl.pallas_call(functools.partial(ladder_kernel, dims), out_shape=(part, p...  26.3 us
    all_gather x1, waiting for transfers between devices, body(): all_cols = lax.all_gather(own_cols, 'cores', axis=0, tiled=True)  26.1 us
    ppermute x8, starting transfers between devices, swap(): return lax.ppermute(array, AXES, [(i, i ^ mask) for i in range(total)])  17.5 us
    all_to_all x1, blocking collectives, body(): every = lax.all_to_all(both, 'node', 0, 0, tiled=True)  11.2 us
    unnamed x21, local copies, waits for them, and re-layouts  5.53 us
  transfers between devices with their start and end apart: 10, of which 9 were waited for; matrix products, arithmetic and copies ran while one was open for 3% of the time, Pallas kernels for 0%

profile of v1, /device:TPU:0, one launch (start us, length us, event | category | flops | bytes accessed | tf_op | source)
XLA Modules:
  0.0 253.9 jit_solution(5962422285378562642)
XLA Ops:
  6.5 1.8 convert_element_type.73
  8.4 0.8 copy.19.tasks_ref
  9.1 81.3 %all-gather.6.cloned.1.call-done = bf16[64,4,64,256]{3,2,1,0:T(8,128)(2,1)} async-done(((bf16[2,4,64,256]{3,2,1,0:T(8,128)(2,1)}), bf16[64,4,64,256]{3,2,1,0:T(8,128)(2,1)}) %all-gather.6.cloned.1.call-update) | async-done | bytes 8388624 | tf_op jit(solution)/shard_map/all_gather | solution.py:177
  90.5 0.7 copy-done.1
  91.1 0.7 copy-done.3
  92.5 26.3 %ladder.1 = (f32[16,256,256]{2,1,0:T(8,128)S(1)}, f32[16,256,256]{2,1,0:T(8,128)}) custom-call(s32[16,32]{1,0:T(8,128)S(1)} %copy-done.3, s32[16,2]{1,0:T(8,128)S(1)} %copy.19.tasks_ref, s32[16]{0:T(128)S(1)} %copy-done.1, s32[4]{0:T(128)S(1)} %copy-done.4, bf16[16,8,256,256]{3,2,1,0:T(8,128)(2,1)} %fitted_ref.1, bf16[32,2,4,64,256]{4,3,2,1,0:T(8,128)(2,1)} %bitcast.60), custom_call_target="tpu_custom_call" | custom-call | flops 40000000000 | bytes 50331648 | tf_op jit(solution)/shard_map/ladder/pallas_call | solution.py:136
  118.8 1.9 copy-done
  120.7 5.5 %collective-permute-start = (f32[16,256,256]{2,1,0:T(8,128)}, f32[16,256,256]{2,1,0:T(8,128)}, u32[]{:S(2)}, u32[]{:S(2)}) collective-permute-start(f32[16,256,256]{2,1,0:T(8,128)} %get-tuple-element.8), channel_id=1, source_target_pairs={{0,8},{1,9},{2,10},{3,11},{4,12},{5,13},{6,14},{7,15},{8,0},{9,1},... | collective-permute-start | bytes 12582920 | tf_op jit(solution)/shard_map/ppermute | solution.py:159
  126.2 7.1 %collective-permute-done = f32[16,256,256]{2,1,0:T(8,128)} collective-permute-done((f32[16,256,256]{2,1,0:T(8,128)}, f32[16,256,256]{2,1,0:T(8,128)}, u32[]{:S(2)}, u32[]{:S(2)}) %collective-permute-start) | collective-permute-done | bytes 4194336 | tf_op jit(solution)/shard_map/ppermute | solution.py:159
  133.4 4.3 %multiply_convert_fusion = f16[16,256,256]{2,1,0:T(8,128)(2,1)S(1)} fusion(f32[16,256,256]{2,1,0:T(8,128)} %copy-done, f32[16,256,256]{2,1,0:T(8,128)} %collective-permute-done), kind=kLoop, calls=%fused_computation | loop fusion | flops 3145728 | bytes 10485760 | tf_op jit(solution)/shard_map/convert_element_type | solution.py:186
  138.3 0.9 constant_dynamic-slice_fusion.3
  139.2 6.8 %collective-permute-start.1 = (f16[8,1,128,256]{3,2,1,0:T(8,128)(2,1)}, f16[8,1,128,256]{3,2,1,0:T(8,128)(2,1)}, u32[]{:S(2)}, u32[]{:S(2)}) collective-permute-start(f16[8,1,128,256]{3,2,1,0:T(8,128)(2,1)} %constant_dynamic-slice_fusion.3), channel_id=1, source_target_pairs={{0,16},{1,17},{2,18},{3,19},{4,20},{5,21},{6,22},{7,23},{8,24},{9,... | collective-permute-start | bytes 1572872 | tf_op jit(solution)/shard_map/ppermute | solution.py:159
  146.3 0.9 copy.30
  147.2 11.4 %collective-permute-done.1 = f16[8,1,128,256]{3,2,1,0:T(8,128)(2,1)} collective-permute-done((f16[8,1,128,256]{3,2,1,0:T(8,128)(2,1)}, f16[8,1,128,256]{3,2,1,0:T(8,128)(2,1)}, u32[]{:S(2)}, u32[]{:S(2)}) %collective-permute-start.1) | collective-permute-done | bytes 524320 | tf_op jit(solution)/shard_map/ppermute | solution.py:159
  158.6 1.2 add_convert_fusion
  159.9 1.2 collective-permute-done.3
  161.3 0.7 collective-permute-start.4
  162.0 5.8 %collective-permute-done.2 = f16[4,128,256]{2,1,0:T(8,128)(2,1)S(1)} collective-permute-done((f16[4,128,256]{2,1,0:T(8,128)(2,1)S(1)}, f16[4,128,256]{2,1,0:T(8,128)(2,1)S(1)}, u32[]{:S(2)}, u32[]{:S(2)}) %collective-permute-start.2) | collective-permute-done | bytes 262176 | tf_op jit(solution)/shard_map/ppermute | solution.py:159
  167.9 0.7 collective-permute-done.4
  168.8 2.5 collective-permute-start.7
  171.3 1.4 collective-permute-start.6
  173.2 3.8 %collective-permute-done.7 = f16[256,256]{1,0:T(8,128)(2,1)S(1)} collective-permute-done((f16[256,256]{1,0:T(8,128)(2,1)S(1)}, f16[256,256]{1,0:T(8,128)(2,1)S(1)}, u32[]{:S(2)}, u32[]{:S(2)}) %collective-permute-start.7) | collective-permute-done | bytes 131104 | tf_op jit(solution)/shard_map/ppermute | solution.py:159
  177.1 5.5 %collective-permute-done.6 = f16[256,256]{1,0:T(8,128)(2,1)S(1)} collective-permute-done((f16[256,256]{1,0:T(8,128)(2,1)S(1)}, f16[256,256]{1,0:T(8,128)(2,1)S(1)}, u32[]{:S(2)}, u32[]{:S(2)}) %collective-permute-start.6) | collective-permute-done | bytes 131104 | tf_op jit(solution)/shard_map/ppermute | solution.py:159
  183.4 11.2 %all_to_all.5 = f32[4,2,64,256]{3,2,1,0:T(8,128)S(1)} all-to-all(f32[4,2,64,256]{3,2,1,0:T(8,128)S(1)} %pad_maximum_fusion), channel_id=1, replica_groups=mesh['node'=4,'cores'=8] {'node'}, dimensions={0} | all-to-all | bytes 1048576 | tf_op jit(solution)/shard_map/all_to_all | solution.py:222
  194.6 0.7 slice.110
  195.5 0.7 fusion.23
  196.7 0.7 fusion.22
  199.5 0.7 fusion.21
  215.3 0.7 fusion.24
  216.1 26.1 %all-gather.4.cloned.1.call-done = f32[16,2,64,256]{3,2,1,0:T(8,128)} async-done(((f32[2,2,64,256]{3,2,1,0:T(8,128)}), f32[16,2,64,256]{3,2,1,0:T(8,128)}) %all-gather.4.cloned.1.call-update) | async-done | bytes 2097168 | tf_op jit(solution)/shard_map/all_gather | solution.py:232
  242.2 3.9 %dynamic-slice_select_fusion.7 = (f32[1,1,64,256]{3,2,1,0:T(8,128)S(1)}, f32[1,1,64,256]{3,2,1,0:T(8,128)S(1)}, f32[1,1,64,256]{3,2,1,0:T(8,128)S(1)}, f32[1,1,6...) fusion(f32[16,2,64,256]{3,2,1,0:T(8,128)} %all-gather.4.cloned., ...), kind=kLoop, calls=%fused_computation.44 | loop fusion | flops 131072 | bytes 1572908 | tf_op jit(solution)/shard_map/jit(_where)/select_n | solution.py:246
  246.3 0.8 copy-done.9
  (50 shorter events, 5.0 us)
Async XLA Ops:
  6.5 84.0 %all-gather.6.cloned.1.call-start = ((), (), s32[]{:S(2)}) async-start(), calls=%async_computation.2 | async-start | bytes 8650752 | tf_op jit(solution)/shard_map/all_gather | solution.py:177
  8.3 233.9 %all-gather.4.cloned.1.call-start = ((), (), s32[]{:S(2)}) async-start(), calls=%async_computation.1 | async-start | bytes 2359296 | tf_op jit(solution)/shard_map/all_gather | solution.py:232
  90.5 0.7 copy-start.1
  91.1 0.7 copy-start.3
  91.8 0.7 copy-start.4
  118.8 2.0 copy-start
  120.7 12.6 %collective-permute-start = (f32[16,256,256]{2,1,0:T(8,128)}, f32[16,256,256]{2,1,0:T(8,128)}, u32[]{:S(2)}, u32[]{:S(2)}) collective-permute-start(f32[16,256,256]{2,1,0:T(8,128)} %get-tuple-element.8), channel_id=1, source_target_pairs={{0,8},{1,9},{2,10},{3,11},{4,12},{5,13},{6,14},{7,15},{8,0},{9,1},... | collective-permute-start | bytes 12582920 | tf_op jit(solution)/shard_map/ppermute | solution.py:159
  139.2 19.4 %collective-permute-start.1 = (f16[8,1,128,256]{3,2,1,0:T(8,128)(2,1)}, f16[8,1,128,256]{3,2,1,0:T(8,128)(2,1)}, u32[]{:S(2)}, u32[]{:S(2)}) collective-permute-start(f16[8,1,128,256]{3,2,1,0:T(8,128)(2,1)} %constant_dynamic-slice_fusion.3), channel_id=1, source_target_pairs={{0,16},{1,17},{2,18},{3,19},{4,20},{5,21},{6,22},{7,23},{8,24},{9,... | collective-permute-start | bytes 1572872 | tf_op jit(solution)/shard_map/ppermute | solution.py:159
  147.2 13.9 %collective-permute-start.3 = (f16[4,2,128,256]{3,2,0,1:T(8,128)(2,1)}, f16[4,2,128,256]{3,2,0,1:T(8,128)(2,1)S(1)}, u32[]{:S(2)}, u32[]{:S(2)}) collective-permute-start(f16[4,2,128,256]{3,2,0,1:T(8,128)(2,1)} %bitcast.52), channel_id=1, source_target_pairs={{0,1},{1,0},{2,3},{3,2},{4,5},{5,4},{6,7},{7,6},{8,9},{9,8},{10,11... | collective-permute-start | bytes 1572872 | tf_op jit(solution)/shard_map/ppermute | solution.py:159
  159.8 7.9 %collective-permute-start.2 = (f16[4,128,256]{2,1,0:T(8,128)(2,1)S(1)}, f16[4,128,256]{2,1,0:T(8,128)(2,1)S(1)}, u32[]{:S(2)}, u32[]{:S(2)}) collective-permute-start(f16[4,128,256]{2,1,0:T(8,128)(2,1)S(1)} %dynamic-slice_bitcast_fusion), channel_id=1, source_target_pairs={{0,1},{1,0},{2,3},{3,2},{4,5},{5,4},{6,7},{7,6},{8,9},{9,8},{10,11... | collective-permute-start | bytes 786440 | tf_op jit(solution)/shard_map/ppermute | solution.py:159
  161.3 7.3 %collective-permute-start.4 = (f16[4,1,128,256]{3,2,0,1:T(8,128)(2,1)S(1)}, f16[4,1,128,256]{3,2,0,1:T(8,128)(2,1)S(1)}, u32[]{:S(2)}, u32[]{:S(2)}) collective-permute-start(f16[4,1,128,256]{3,2,0,1:T(8,128)(2,1)S(1)} %constant_dynamic-slice_fusion), channel_id=1, source_target_pairs={{0,16},{1,17},{2,18},{3,19},{4,20},{5,21},{6,22},{7,23},{8,24},{9,... | collective-permute-start | bytes 786440 | tf_op jit(solution)/shard_map/ppermute | solution.py:159
  162.0 33.4 %copy-start.2 = (s32[16]{0:T(128)S(1)}, s32[16]{0:T(128)}, u32[]{:S(2)}) copy-start(s32[16]{0:T(128)} %owner_ref.1) | copy-start | bytes 196
  162.0 39.6 %copy-start.5 = (s32[4]{0:T(128)S(1)}, s32[4]{0:T(128)}, u32[]{:S(2)}) copy-start(s32[4]{0:T(128)} %partner_ref.1) | copy-start | bytes 52
  167.8 47.4 %copy-start.7 = (f32[1024]{0:T(1024)S(1)}, f32[1024]{0:T(1024)}, u32[]{:S(2)}) copy-start(f32[1024]{0:T(1024)} %param.15) | copy-start | bytes 12292
  167.8 48.2 %copy-start.8 = (f32[4]{0:T(128)S(1)}, f32[4]{0:T(128)}, u32[]{:S(2)}) copy-start(f32[4]{0:T(128)} %param.14) | copy-start | bytes 52
  168.8 8.3 %collective-permute-start.7 = (f16[256,256]{1,0:T(8,128)(2,1)S(1)}, f16[256,256]{1,0:T(8,128)(2,1)S(1)}, u32[]{:S(2)}, u32[]{:S(2)}) collective-permute-start(f16[256,256]{1,0:T(8,128)(2,1)S(1)} %get-tuple-element.33), channel_id=1, source_target_pairs={{0,6},{1,7},{2,4},{3,5},{4,2},{5,3},{6,0},{7,1},{8,14},{9,15},{10,... | collective-permute-start | bytes 393224 | tf_op jit(solution)/shard_map/ppermute | solution.py:159
  171.3 11.2 %collective-permute-start.6 = (f16[256,256]{1,0:T(8,128)(2,1)S(1)}, f16[256,256]{1,0:T(8,128)(2,1)S(1)}, u32[]{:S(2)}, u32[]{:S(2)}) collective-permute-start(f16[256,256]{1,0:T(8,128)(2,1)S(1)} %get-tuple-element.32), channel_id=1, source_target_pairs={{0,4},{1,5},{2,6},{3,7},{4,0},{5,1},{6,2},{7,3},{8,12},{9,13},{10,... | collective-permute-start | bytes 393224 | tf_op jit(solution)/shard_map/ppermute | solution.py:159
  172.7 9.8 %collective-permute-start.5 = (f16[256,256]{1,0:T(8,128)(2,1)S(1)}, f16[256,256]{1,0:T(8,128)(2,1)S(1)}, u32[]{:S(2)}, u32[]{:S(2)}) collective-permute-start(f16[256,256]{1,0:T(8,128)(2,1)S(1)} %get-tuple-element.31), channel_id=1, source_target_pairs={{0,2},{1,3},{2,0},{3,1},{4,6},{5,7},{6,4},{7,5},{8,10},{9,11},{10,... | collective-permute-start | bytes 393224 | tf_op jit(solution)/shard_map/ppermute | solution.py:159
  173.2 72.8 %copy-start.6 = (f32[2,4,64,256]{3,2,1,0:T(8,128)S(1)}, f32[2,4,64,256]{3,2,1,0:T(8,128)}, u32[]{:S(2)}) copy-start(f32[2,4,64,256]{3,2,1,0:T(8,128)} %param.13) | copy-start | bytes 1572868
  246.2 0.8 copy-start.9
Sparse Core Ops, SparseCore 0:
  10.3 80.1 all-gather.5
  195.5 46.6 all-gather.3

commit v2 on v1

v2 whole, which is shorter than its diff:
```python
import functools
import math

import jax
import jax.numpy as jnp
from jax import lax
from jax.experimental import pallas as pl
from jax.experimental.pallas import tpu as pltpu
from jax.sharding import PartitionSpec as P

AXES = ("node", "cores")


def ladder_kernel(
    dims, mask_ref, tasks_ref, owner_ref, fitted_ref, amps_ref, keep_ref, send_ref,
    left_buf, right_buf, half_buf, tile_buf, total, work, slot_of, load_sems, store_sems,
):
    nodes, cores, slots_here, rows, tile, aux, slots, side = dims
    task_count = tasks_ref.shape[0]
    node_index = lax.axis_index("node")
    core_index = lax.axis_index("cores")
    block = node_index * cores + core_index

    def invert(s, carry):
        slot_of[owner_ref[s]] = s
        return carry

    lax.fori_loop(0, slots, invert, 0)

    def indices(t):
        out_tile = tasks_ref[t, 0]
        in_tile = tasks_ref[t, 1]
        a, b = out_tile // side, out_tile % side
        c, d = in_tile // side, in_tile % side
        return a, b, a * side + c, b * side + d, in_tile

    def enlist(t, count):
        _, _, left, right, _ = indices(t)
        work[count] = t
        return count + mask_ref[left, block] * mask_ref[right, block]

    active = lax.fori_loop(0, task_count, enlist, jnp.int32(0))

    def loads(i, slot):
        _, _, left, right, in_tile = indices(work[i])
        place = slot_of[in_tile]
        owner = place // slots_here
        inside = place % slots_here
        copies = [pltpu.make_async_copy(fitted_ref.at[left], left_buf.at[slot], load_sems.at[slot, 0])]
        for q in range(aux):
            copies.append(
                pltpu.make_async_copy(
                    fitted_ref.at[right, q], right_buf.at[slot, :, pl.ds(q * tile, tile)], load_sems.at[slot, 1]
                )
            )
        for n in range(nodes):
            copies.append(
                pltpu.make_async_copy(
                    amps_ref.at[n * cores + owner, inside],
                    tile_buf.at[slot, :, pl.ds(n * rows, rows), :],
                    load_sems.at[slot, 2],
                )
            )
        return copies

    @pl.when(active > 0)
    def _():
        for copy in loads(0, 0):
            copy.start()

    @pl.loop(0, slots)
    def _(s):
        total[s] = jnp.zeros(total.shape[1:], jnp.float32)

    def contract(first, second):
        return lax.dot_general(first, second, (((1,), (1,)), ((), ())), preferred_element_type=jnp.float32)

    @pl.loop(0, active)
    def _(i):
        slot = i % 2

        @pl.when(i + 1 < active)
        def _():
            for copy in loads(i + 1, 1 - slot):
                copy.start()

        for copy in loads(i, slot):
            copy.wait()
        a, b, _, _, _ = indices(work[i])
        straight = slot_of[a * side + b]
        crossed = slot_of[b * side + a]
        left_all = left_buf[slot].reshape(aux * tile, tile)
        for p in range(2):
            half = jnp.dot(left_all, tile_buf[slot, p], preferred_element_type=jnp.float32).astype(jnp.bfloat16)
            for q in range(aux):
                half_buf[p, :, q * tile:(q + 1) * tile] = half[q * tile:(q + 1) * tile]
        shape = total.shape[1:]
        total[straight] += contract(half_buf[0], right_buf[slot]).reshape(shape)
        total[crossed] += contract(right_buf[slot], half_buf[1]).reshape(shape)

    mine = node_index % 2
    stores = [
        pltpu.make_async_copy(total.at[:, :, mine], keep_ref, store_sems.at[0]),
        pltpu.make_async_copy(total.at[:, :, 1 - mine], send_ref, store_sems.at[1]),
    ]
    for copy in stores:
        copy.start()
    for copy in stores:
        copy.wait()


def ladder_terms(mask, tasks, owner_map, fitted, gathered, nodes, cores):
    tile_pairs, aux, tile, _ = fitted.shape
    slots_here, _, rows = gathered.shape[1:4]
    side = math.isqrt(tile_pairs)
    dims = (nodes, cores, slots_here, rows, tile, aux, tile_pairs, side)
    smem = pl.BlockSpec(memory_space=pltpu.SMEM)
    hbm = pl.BlockSpec(memory_space=pl.ANY)
    part = jax.ShapeDtypeStruct((tile_pairs, nodes // 2, rows, tile), jnp.float32)
    return pl.pallas_call(
        functools.partial(ladder_kernel, dims),
        out_shape=(part, part),
        in_specs=[smem, smem, smem, hbm, hbm],
        out_specs=(hbm, hbm),
        scratch_shapes=[
            pltpu.VMEM((2, aux, tile, tile), jnp.bfloat16),
            pltpu.VMEM((2, tile, aux * tile), jnp.bfloat16),
            pltpu.VMEM((2, tile, aux * tile), jnp.bfloat16),
            pltpu.VMEM((2, 2, tile, tile), jnp.bfloat16),
            pltpu.VMEM((tile_pairs, nodes // 2, 2, rows, tile), jnp.float32),
            pltpu.SMEM((tasks.shape[0] + 1,), jnp.int32),
            pltpu.SMEM((tile_pairs,), jnp.int32),
            pltpu.SemaphoreType.DMA((2, 3)),
            pltpu.SemaphoreType.DMA((2,)),
        ],
        compiler_params=pltpu.CompilerParams(vmem_limit_bytes=32 * 1024 * 1024),
        cost_estimate=pl.CostEstimate(flops=20 * 10**9, bytes_accessed=30 * 2**20, transcendentals=0),
        name="ladder",
    )(mask, tasks, owner_map, fitted, gathered)


def swap(array, mask, total):
    return lax.ppermute(array, AXES, [(i, i ^ mask) for i in range(total)])


def pick(array, index, axis):
    return lax.dynamic_index_in_dim(array, index, axis, keepdims=False)


def halve(value, index, axis, mask, total):
    shape = value.shape
    split = value.reshape(shape[:axis] + (shape[axis] // 2, 2) + shape[axis + 1:])
    other = swap(pick(split, 1 - index, axis + 1), mask, total)
    own = pick(split, index, axis + 1)
    return (own.astype(jnp.float32) + other.astype(jnp.float32)).astype(value.dtype)


def reduce_blocks(keep, send, nodes, cores, scale):
    total = nodes * cores
    node_index = lax.axis_index("node")
    core_index = lax.axis_index("cores")
    slots, inner, rows, tile = keep.shape
    got = swap(send, cores, total)
    part = ((keep + got) * scale).astype(jnp.float16).reshape(cores, slots // cores, inner, rows, tile)

    def over_inner(value):
        mask, index = 2 * cores, node_index // 2
        while value.shape[2] > 1:
            value = halve(value, index % 2, 2, mask, total)
            mask, index = mask * 2, index // 2
        return value

    def over_low(value):
        return halve(value, core_index % 2, 0, 1, total)

    upper = over_low(over_inner(part[:, :, :, :rows // 2]))
    lower = over_inner(over_low(part[:, :, :, rows // 2:]))
    part = jnp.concatenate([upper, lower], axis=3)[:, :, 0]
    at = core_index // 2
    mine = pick(part, at, 0).astype(jnp.float32)
    for step in range(1, part.shape[0]):
        mine = mine + swap(pick(part, at ^ step, 0), 2 * step, total).astype(jnp.float32)
    return mine * (0.5 / scale)


def turn_blocks(mine, nodes, cores, scale):
    total = nodes * cores
    slots_here, rows, tile = mine.shape
    node_index = lax.axis_index("node")
    turned = (mine * scale).astype(jnp.float16).reshape(slots_here * rows, tile).T
    turned = turned.reshape(nodes, rows, slots_here * rows)
    pieces = [swap(pick(turned, node_index ^ step, 0), step * cores, total) for step in range(1, nodes)]
    pieces = jnp.stack([pick(turned, node_index, 0)] + pieces)
    every = lax.all_gather(pieces, "cores", axis=0, tiled=False)
    return every


def strips(every, place, node_index, slots_here, scale):
    _, nodes, rows, width = every.shape
    owner, inside = place // slots_here, place % slots_here
    block = pick(every, owner, 0).reshape(nodes, rows, slots_here, width // slots_here)
    block = pick(block, inside, 2).astype(jnp.float32) * (1.0 / scale)
    ordered = [pick(block, node_index ^ n, 0) for n in range(nodes)]
    return jnp.concatenate(ordered, axis=1)


def body(nodes, cores, fitted, fit_mask, tasks, owner_map, partner, amplitudes, pair_energy, virt_energy):
    slots_here, pairs, rows, tile = amplitudes.shape
    tile_pairs = owner_map.shape[0]
    side = math.isqrt(tile_pairs)
    node_index = lax.axis_index("node")
    core_index = lax.axis_index("cores")
    scale = 2.0 ** -9

    pair_ids = jnp.arange(pairs, dtype=jnp.int32)
    is_rep = pair_ids < partner
    low = jnp.minimum(pair_ids, partner)
    ranks = jnp.sum((is_rep[None, :] & (pair_ids[None, :] < low[:, None])).astype(jnp.int32), axis=1)
    groups = pairs // 2
    pair_of = [jnp.sum(jnp.where(is_rep & (ranks == g), pair_ids, 0)) for g in range(groups)]
    twin_of = [jnp.sum(jnp.where(~is_rep & (ranks == g), pair_ids, 0)) for g in range(groups)]
    places = jnp.arange(tile_pairs, dtype=jnp.int32)
    slot_of = jnp.sum(jnp.where(owner_map[None, :] == places[:, None], places[None, :], 0), axis=1)
    my_tiles = lax.dynamic_slice_in_dim(owner_map, core_index * slots_here, slots_here)
    row_tiles, col_tiles = my_tiles // side, my_tiles % side

    gathered = []
    for g in range(groups):
        chosen = jnp.stack([pick(amplitudes, pair_of[g], 1), pick(amplitudes, twin_of[g], 1)], axis=1)
        lowered = chosen.astype(jnp.bfloat16)
        if gathered:
            lowered, gathered[-1] = lax.optimization_barrier((lowered, gathered[-1]))
        gathered.append(lax.all_gather(lowered, AXES, axis=0, tiled=False))
    straight, crossed = [], []
    for g in range(groups):
        keep, send = ladder_terms(fit_mask, tasks, owner_map, fitted, gathered[g], nodes, cores)
        mine = reduce_blocks(keep, send, nodes, cores, scale)
        straight.append(mine)
        crossed.append(turn_blocks(mine, nodes, cores, scale))
    out = []
    for j in range(slots_here):
        place = slot_of[col_tiles[j] * side + row_tiles[j]]
        turned = [strips(crossed[g], place, node_index, slots_here, scale) for g in range(groups)]
        symmetric = []
        for p in range(pairs):
            same = straight[0][j]
            other = turned[0]
            for g in range(1, groups):
                same = jnp.where(ranks[p] == g, straight[g][j], same)
                other = jnp.where(ranks[p] == g, turned[g], other)
            symmetric.append(jnp.where(is_rep[p], same, other))
        row_energy = lax.dynamic_slice_in_dim(virt_energy, row_tiles[j] * tile + node_index * rows, rows)
        col_energy = lax.dynamic_slice_in_dim(virt_energy, col_tiles[j] * tile, tile)
        denominator = (pair_energy[:, None, None] - row_energy[None, :, None]) - col_energy[None, None, :]
        out.append(amplitudes[j] + jnp.stack(symmetric) / denominator)
    return jnp.stack(out)


def solution(mesh):
    placed = (P(None, AXES, None, None), P(), P(), P(), P(), P("cores", None, "node", None), P(), P())
    return jax.shard_map(
        functools.partial(body, mesh.shape["node"], mesh.shape["cores"]),
        mesh=mesh, in_specs=placed, out_specs=P("cores", None, "node", None), check_vma=False,
    )
```

time: 256 us -> 311 us (1.21)
  blocking collectives: 11.2 us -> 62.6 us
  waiting for transfers between devices: 143 us -> 115 us
  starting transfers between devices: 17.5 us -> 36.8 us
  other arithmetic: 12.3 us -> 18 us
  between operations: 30.4 us -> 34.5 us
    all_gather x0 -> x2, blocking collectives: none -> 62.6 us  [turn_blocks(): every = lax.all_gather(pieces, 'cores', axis=0, tiled=False)]
    ppermute x8 -> x22, waiting for transfers between devices: 35.5 us -> 13.1 us  [swap(): return lax.ppermute(array, AXES, [(i, i ^ mask) for i in range(total)])]
    ppermute x8 -> x22, starting transfers between devices: 17.5 us -> 36.7 us  [swap(): return lax.ppermute(array, AXES, [(i, i ^ mask) for i in range(total)])]
    all_to_all x1 -> x0, blocking collectives: 11.2 us -> none  [body(): every = lax.all_to_all(both, 'node', 0, 0, tiled=True)]
    another operation x1 -> x8, other arithmetic: 0.04 us -> 6.85 us  [the longest x4 5.48 us: body(): out.append(amplitudes[j] + jnp.stack(symmetric) / denominator)]
    all_gather x2, waiting for transfers between devices: 107 us -> 102 us  [body(): gathered.append(lax.all_gather(lowered, AXES, axis=0, tiled=False))]
    select_n x1 -> x0, other arithmetic: 3.85 us -> none  [body(): jnp.where(is_rep[p], pick(own_rows[j], ranks[p], 0), pick(crossed, ranks[...]
    unnamed x21 -> x27, local copies, waits for them, and re-layouts: 5.53 us -> 8.79 us
  transfers between devices with their start and end apart: 10 -> 24, of which waited for: 9 -> 8; matrix products, arithmetic and copies ran while one was open for 3% -> 5% of each run, Pallas kernels for 0% -> 8%
where the time goes in v2:
time: 311 us; the launch traced here: 308 us
  waiting for transfers between devices  115 us (37%)
  blocking collectives  62.6 us (20%)
  starting transfers between devices  36.8 us (12%)
  between operations  34.5 us (11%)
  Pallas kernels  25.9 us (8%)
  other arithmetic  18 us (6%)
  local copies, waits for them, and re-layouts  15.3 us (5%)
    all_gather x2, waiting for transfers between devices, body(): gathered.append(lax.all_gather(lowered, AXES, axis=0, tiled=False))  102 us
    all_gather x2, blocking collectives, turn_blocks(): every = lax.all_gather(pieces, 'cores', axis=0, tiled=False)  62.6 us
    ppermute x22, starting transfers between devices, swap(): return lax.ppermute(array, AXES, [(i, i ^ mask) for i in range(total)])  36.7 us
    pallas_call x2, Pallas kernels, ladder_terms(): pl.pallas_call(functools.partial(ladder_kernel, dims), out_shape=(part, p...  25.9 us
    ppermute x22, waiting for transfers between devices, swap(): return lax.ppermute(array, AXES, [(i, i ^ mask) for i in range(total)])  13.1 us
    unnamed x27, local copies, waits for them, and re-layouts  8.79 us
  transfers between devices with their start and end apart: 24, of which 8 were waited for; matrix products, arithmetic and copies ran while one was open for 5% of the time, Pallas kernels for 8%

profile of v2, /device:TPU:0, one launch (start us, length us, event | category | flops | bytes accessed | tf_op | source)
XLA Modules:
  0.0 308.4 jit_solution(14130875750240259933)
XLA Ops:
  8.0 1.4 fusion.37
  17.1 1.1 fusion.10
  19.6 64.2 %all-gather.6.cloned.1.call-done.amps_ref = bf16[32,2,2,64,256]{4,3,2,1,0:T(8,128)(2,1)} async-done(((bf16[1,2,2,64,256]{4,3,2,1,0:T(8,128)(2,1)}), bf16[32,2,2,64,256]{4,3,2,1,0:T(8,128)(2,1)}) %all-gather.6.cloned.1.call-update) | async-done | bytes 4194320 | tf_op jit(solution)/shard_map/all_gather | solution.py:233
  86.1 2.2 copy-done.3
  89.0 13.0 %ladder.3 = (f32[16,2,64,256]{3,2,1,0:T(8,128)S(1)}, f32[16,2,64,256]{3,2,1,0:T(8,128)}) custom-call(s32[16,32]{1,0:T(8,128)S(1)} %copy-done.5, s32[16,2]{1,0:T(8,128)S(1)} %copy.41.tasks_ref, s32[16]{0:T(128)S(1)} %copy-done.1, bf16[16,8,256,256]{3,2,1,0:T(8,128)(2,1)} %fitted_ref.3, bf16[32,2,2,64,256]{4,3,2,1,0:T(8,128)(2,1)S(1)} %copy-done.3), custom_call_target="tpu_custom_call" | custom-call | flops 20000000000 | bytes 31457280 | tf_op jit(solution)/shard_map/ladder/pallas_call | solution.py:120
  102.0 1.4 copy-done
  103.4 6.2 %collective-permute-start.8 = (f32[16,2,64,256]{3,2,1,0:T(8,128)}, f32[16,2,64,256]{3,2,1,0:T(8,128)}, u32[]{:S(2)}, u32[]{:S(2)}) collective-permute-start(f32[16,2,64,256]{3,2,1,0:T(8,128)} %get-tuple-element.16), channel_id=1, source_target_pairs={{0,8},{1,9},{2,10},{3,11},{4,12},{5,13},{6,14},{7,15},{8,0},{9,1},... | collective-permute-start | bytes 6291464 | tf_op jit(solution)/shard_map/ppermute | solution.py:143
  109.6 38.0 %all-gather.8.cloned.1.call-done = bf16[64,2,64,256]{3,2,1,0:T(8,128)(2,1)} async-done(((bf16[2,2,64,256]{3,2,1,0:T(8,128)(2,1)}), bf16[64,2,64,256]{3,2,1,0:T(8,128)(2,1)}) %all-gather.8.cloned.1.call-update) | async-done | bytes 4194320 | tf_op jit(solution)/shard_map/all_gather | solution.py:233
  147.5 2.2 copy-done.4
  149.7 12.9 %ladder.2 = (f32[16,2,64,256]{3,2,1,0:T(8,128)S(1)}, f32[16,2,64,256]{3,2,1,0:T(8,128)}) custom-call(s32[16,32]{1,0:T(8,128)S(1)} %copy-done.6, s32[16,2]{1,0:T(8,128)S(1)} %copy.41.tasks_ref, s32[16]{0:T(128)S(1)} %copy-done.2, bf16[16,8,256,256]{3,2,1,0:T(8,128)(2,1)} %fitted_ref.3, bf16[32,2,2,64,256]{4,3,2,1,0:T(8,128)(2,1)S(1)} %bitcast.169), custom_call_target="tpu_custom_call" | custom-call | flops 20000000000 | bytes 31457280 | tf_op jit(solution)/shard_map/ladder/pallas_call | solution.py:120
  162.6 6.3 %collective-permute-start = (f32[16,2,64,256]{3,2,1,0:T(8,128)}, f32[16,2,64,256]{3,2,1,0:T(8,128)}, u32[]{:S(2)}, u32[]{:S(2)}) collective-permute-start(f32[16,2,64,256]{3,2,1,0:T(8,128)} %get-tuple-element.13), channel_id=1, source_target_pairs={{0,8},{1,9},{2,10},{3,11},{4,12},{5,13},{6,14},{7,15},{8,0},{9,1},... | collective-permute-start | bytes 6291464 | tf_op jit(solution)/shard_map/ppermute | solution.py:143
  174.2 2.7 multiply_convert_fusion
  177.3 2.8 collective-permute-start.9
  191.2 1.0 add_convert_fusion
  192.3 5.1 %collective-permute-start.10 = (f16[4,2,1,32,256]{4,3,1,2,0:T(8,128)(2,1)S(1)}, f16[4,2,1,32,256]{4,3,1,2,0:T(8,128)(2,1)S(1)}, u32[]{:S(2)}, u32[]{:S(2)}) collective-permute-start(f16[4,2,1,32,256]{4,3,1,2,0:T(8,128)(2,1)S(1)} %dynamic-slice_bitcast_fusion.2), channel_id=1, source_target_pairs={{0,1},{1,0},{2,3},{3,2},{4,5},{5,4},{6,7},{7,6},{8,9},{9,8},{10,11... | collective-permute-start | bytes 393224 | tf_op jit(solution)/shard_map/ppermute | solution.py:143
  197.4 2.1 multiply_convert_fusion.1
  200.2 1.0 collective-permute-done.10
  201.8 1.8 collective-permute-start.3
  203.6 5.8 %collective-permute-done.11 = f16[4,2,2,32,256]{4,3,1,2,0:T(8,128)(2,1)S(1)} collective-permute-done((f16[4,2,2,32,256]{4,3,1,2,0:T(8,128)(2,1)S(1)}, f16[4,2,2,32,256]{4,3,1,2,0:T(8,128)(2,1)S(1)}, u32[]{:S(2)}, u32[]{:S(2)}) %collective-permute-start.11) | collective-permute-done | bytes 262176 | tf_op jit(solution)/shard_map/ppermute | solution.py:143
  209.8 1.2 collective-permute-start.2
  211.0 4.0 %collective-permute-done.3 = f16[4,2,2,32,256]{4,3,1,0,2:T(8,128)(2,1)S(1)} collective-permute-done((f16[4,2,2,32,256]{4,3,1,0,2:T(8,128)(2,1)S(1)}, f16[4,2,2,32,256]{4,3,1,0,2:T(8,128)(2,1)S(1)}, u32[]{:S(2)}, u32[]{:S(2)}) %collective-permute-start.3) | collective-permute-done | bytes 262176 | tf_op jit(solution)/shard_map/ppermute | solution.py:143
  215.4 3.7 %collective-permute-start.15 = (f16[2,64,256]{2,1,0:T(8,128)(2,1)S(1)}, f16[2,64,256]{2,1,0:T(8,128)(2,1)S(1)}, u32[]{:S(2)}, u32[]{:S(2)}) collective-permute-start(f16[2,64,256]{2,1,0:T(8,128)(2,1)S(1)} %get-tuple-element.62), channel_id=1, source_target_pairs={{0,6},{1,7},{2,4},{3,5},{4,2},{5,3},{6,0},{7,1},{8,14},{9,15},{10,... | collective-permute-start | bytes 196616 | tf_op jit(solution)/shard_map/ppermute | solution.py:143
  220.3 3.4 %collective-permute-start.7 = (f16[2,64,256]{2,1,0:T(8,128)(2,1)S(1)}, f16[2,64,256]{2,1,0:T(8,128)(2,1)S(1)}, u32[]{:S(2)}, u32[]{:S(2)}) collective-permute-start(f16[2,64,256]{2,1,0:T(8,128)(2,1)S(1)} %get-tuple-element.59), channel_id=1, source_target_pairs={{0,6},{1,7},{2,4},{3,5},{4,2},{5,3},{6,0},{7,1},{8,14},{9,15},{10,... | collective-permute-start | bytes 196616 | tf_op jit(solution)/shard_map/ppermute | solution.py:143
  223.7 1.0 collective-permute-start.5
  224.8 1.1 collective-permute-done.14
  226.2 1.5 collective-permute-start.20
  228.0 0.9 collective-permute-done.6
  229.4 1.1 collective-permute-start.17
  231.1 31.3 %all-gather.2 = f16[32,64,128]{2,1,0:T(8,128)(2,1)S(1)} all-gather(f16[4,64,128]{2,1,0:T(8,128)(2,1)S(1)} %pad_maximum_fusion.5), channel_id=4, replica_groups=mesh['node'=4,'cores'=8] {'cores'}, dimensions={0}, use_global_device_ids=true | all-gather | bytes 589824 | tf_op jit(solution)/shard_map/all_gather | solution.py:194
  262.8 31.3 %all-gather.1 = f16[32,64,128]{2,1,0:T(8,128)(2,1)S(1)} all-gather(f16[4,64,128]{2,1,0:T(8,128)(2,1)S(1)} %pad_maximum_fusion.3), channel_id=3, replica_groups=mesh['node'=4,'cores'=8] {'cores'}, dimensions={0}, use_global_device_ids=true | all-gather | bytes 589824 | tf_op jit(solution)/shard_map/all_gather | solution.py:194
  295.8 2.0 select_bitcast_fusion.6
  298.6 2.0 select_bitcast_fusion.2
  (116 shorter events, 18.2 us)
Async XLA Ops:
  6.5 77.3 %all-gather.6.cloned.1.call-start = ((), (), s32[]{:S(2)}) async-start(), calls=%async_computation | async-start | bytes 4325376 | tf_op jit(solution)/shard_map/all_gather | solution.py:233
  18.9 128.6 %all-gather.8.cloned.1.call-start = ((), (), s32[]{:S(2)}) async-start(), calls=%async_computation.1 | async-start | bytes 4325376 | tf_op jit(solution)/shard_map/all_gather | solution.py:233
  86.1 2.2 copy-start.3
  89.0 58.6 %copy-start.2 = (s32[16]{0:T(128)S(1)}, s32[16]{0:T(128)}, u32[]{:S(2)}) copy-start(s32[16]{0:T(128)} %owner_ref.3) | copy-start | bytes 196
  89.0 58.6 %copy-start.6 = (s32[16,32]{1,0:T(8,128)S(1)}, s32[16,32]{1,0:T(8,128)}, u32[]{:S(2)}) copy-start(s32[16,32]{1,0:T(8,128)} %mask_ref.3) | copy-start | bytes 6148
  103.4 70.9 %collective-permute-start.8 = (f32[16,2,64,256]{3,2,1,0:T(8,128)}, f32[16,2,64,256]{3,2,1,0:T(8,128)}, u32[]{:S(2)}, u32[]{:S(2)}) collective-permute-start(f32[16,2,64,256]{3,2,1,0:T(8,128)} %get-tuple-element.16), channel_id=1, source_target_pairs={{0,8},{1,9},{2,10},{3,11},{4,12},{5,13},{6,14},{7,15},{8,0},{9,1},... | collective-permute-start | bytes 6291464 | tf_op jit(solution)/shard_map/ppermute | solution.py:143
  147.5 2.2 copy-start.4
  149.7 22.9 %copy-start.8 = (f32[1024]{0:T(1024)S(1)}, f32[1024]{0:T(1024)}, u32[]{:S(2)}) copy-start(f32[1024]{0:T(1024)} %param.15) | copy-start | bytes 12292
  162.6 34.8 %collective-permute-start = (f32[16,2,64,256]{3,2,1,0:T(8,128)}, f32[16,2,64,256]{3,2,1,0:T(8,128)}, u32[]{:S(2)}, u32[]{:S(2)}) collective-permute-start(f32[16,2,64,256]{3,2,1,0:T(8,128)} %get-tuple-element.13), channel_id=1, source_target_pairs={{0,8},{1,9},{2,10},{3,11},{4,12},{5,13},{6,14},{7,15},{8,0},{9,1},... | collective-permute-start | bytes 6291464 | tf_op jit(solution)/shard_map/ppermute | solution.py:143
  176.9 14.2 %copy-start.9 = (f32[4]{0:T(128)S(1)}, f32[4]{0:T(128)}, u32[]{:S(2)}) copy-start(f32[4]{0:T(128)} %param.14) | copy-start | bytes 52
  177.3 13.9 %collective-permute-start.9 = (f16[8,2,1,32,256]{4,3,1,0,2:T(8,128)(2,1)S(1)}, f16[8,2,1,32,256]{4,3,1,0,2:T(8,128)(2,1)}, u32[]{:S(2)}, u32[]{:S(2)}) collective-permute-start(f16[8,2,1,32,256]{4,3,1,0,2:T(8,128)(2,1)S(1)} %dynamic-slice_bitcast_fusion), channel_id=1, source_target_pairs={{0,16},{1,17},{2,18},{3,19},{4,20},{5,21},{6,22},{7,23},{8,24},{9,... | collective-permute-start | bytes 786440 | tf_op jit(solution)/shard_map/ppermute | solution.py:143
  192.3 9.0 %collective-permute-start.10 = (f16[4,2,1,32,256]{4,3,1,2,0:T(8,128)(2,1)S(1)}, f16[4,2,1,32,256]{4,3,1,2,0:T(8,128)(2,1)S(1)}, u32[]{:S(2)}, u32[]{:S(2)}) collective-permute-start(f16[4,2,1,32,256]{4,3,1,2,0:T(8,128)(2,1)S(1)} %dynamic-slice_bitcast_fusion.2), channel_id=1, source_target_pairs={{0,1},{1,0},{2,3},{3,2},{4,5},{5,4},{6,7},{7,6},{8,9},{9,8},{10,11... | collective-permute-start | bytes 393224 | tf_op jit(solution)/shard_map/ppermute | solution.py:143
  200.1 9.2 %collective-permute-start.11 = (f16[4,2,2,32,256]{4,3,1,2,0:T(8,128)(2,1)S(1)}, f16[4,2,2,32,256]{4,3,1,2,0:T(8,128)(2,1)S(1)}, u32[]{:S(2)}, u32[]{:S(2)}) collective-permute-start(f16[4,2,2,32,256]{4,3,1,2,0:T(8,128)(2,1)S(1)} %bitcast.183), channel_id=1, source_target_pairs={{0,1},{1,0},{2,3},{3,2},{4,5},{5,4},{6,7},{7,6},{8,9},{9,8},{10,11... | collective-permute-start | bytes 786440 | tf_op jit(solution)/shard_map/ppermute | solution.py:143
  201.4 8.2 %collective-permute-start.1 = (f16[8,2,1,32,256]{4,3,1,0,2:T(8,128)(2,1)S(1)}, f16[8,2,1,32,256]{4,3,1,0,2:T(8,128)(2,1)S(1)}, u32[]{:S(2)}, u32[]{:S(2)}) collective-permute-start(f16[8,2,1,32,256]{4,3,1,0,2:T(8,128)(2,1)S(1)} %dynamic-slice_bitcast_fusion.1), channel_id=1, source_target_pairs={{0,16},{1,17},{2,18},{3,19},{4,20},{5,21},{6,22},{7,23},{8,24},{9,... | collective-permute-start | bytes 786440 | tf_op jit(solution)/shard_map/ppermute | solution.py:143
  201.8 13.2 %collective-permute-start.3 = (f16[4,2,2,32,256]{4,3,1,0,2:T(8,128)(2,1)S(1)}, f16[4,2,2,32,256]{4,3,1,0,2:T(8,128)(2,1)S(1)}, u32[]{:S(2)}, u32[]{:S(2)}) collective-permute-start(f16[4,2,2,32,256]{4,3,1,0,2:T(8,128)(2,1)S(1)} %bitcast.182), channel_id=1, source_target_pairs={{0,1},{1,0},{2,3},{3,2},{4,5},{5,4},{6,7},{7,6},{8,9},{9,8},{10,11... | collective-permute-start | bytes 786440 | tf_op jit(solution)/shard_map/ppermute | solution.py:143
  209.5 5.7 %collective-permute-start.12 = (f16[4,2,1,32,256]{4,3,1,2,0:T(8,128)(2,1)S(1)}, f16[4,2,1,32,256]{4,3,1,2,0:T(8,128)(2,1)S(1)}, u32[]{:S(2)}, u32[]{:S(2)}) collective-permute-start(f16[4,2,1,32,256]{4,3,1,2,0:T(8,128)(2,1)S(1)} %constant_dynamic-slice_fusion.28), channel_id=1, source_target_pairs={{0,16},{1,17},{2,18},{3,19},{4,20},{5,21},{6,22},{7,23},{8,24},{9,... | collective-permute-start | bytes 393224 | tf_op jit(solution)/shard_map/ppermute | solution.py:143
  209.8 10.0 %collective-permute-start.2 = (f16[4,2,1,32,256]{4,3,1,0,2:T(8,128)(2,1)S(1)}, f16[4,2,1,32,256]{4,3,1,0,2:T(8,128)(2,1)S(1)}, u32[]{:S(2)}, u32[]{:S(2)}) collective-permute-start(f16[4,2,1,32,256]{4,3,1,0,2:T(8,128)(2,1)S(1)} %dynamic-slice_bitcast_fusion.3), channel_id=1, source_target_pairs={{0,1},{1,0},{2,3},{3,2},{4,5},{5,4},{6,7},{7,6},{8,9},{9,8},{10,11... | collective-permute-start | bytes 393224 | tf_op jit(solution)/shard_map/ppermute | solution.py:143
  215.2 5.0 %collective-permute-start.4 = (f16[4,2,1,32,256]{4,3,1,0,2:T(8,128)(2,1)S(1)}, f16[4,2,1,32,256]{4,3,1,0,2:T(8,128)(2,1)S(1)}, u32[]{:S(2)}, u32[]{:S(2)}) collective-permute-start(f16[4,2,1,32,256]{4,3,1,0,2:T(8,128)(2,1)S(1)} %constant_dynamic-slice_fusion.31), channel_id=1, source_target_pairs={{0,16},{1,17},{2,18},{3,19},{4,20},{5,21},{6,22},{7,23},{8,24},{9,... | collective-permute-start | bytes 393224 | tf_op jit(solution)/shard_map/ppermute | solution.py:143
  215.4 8.3 %collective-permute-start.15 = (f16[2,64,256]{2,1,0:T(8,128)(2,1)S(1)}, f16[2,64,256]{2,1,0:T(8,128)(2,1)S(1)}, u32[]{:S(2)}, u32[]{:S(2)}) collective-permute-start(f16[2,64,256]{2,1,0:T(8,128)(2,1)S(1)} %get-tuple-element.62), channel_id=1, source_target_pairs={{0,6},{1,7},{2,4},{3,5},{4,2},{5,3},{6,0},{7,1},{8,14},{9,15},{10,... | collective-permute-start | bytes 196616 | tf_op jit(solution)/shard_map/ppermute | solution.py:143
  219.1 6.8 %collective-permute-start.14 = (f16[2,64,256]{2,1,0:T(8,128)(2,1)S(1)}, f16[2,64,256]{2,1,0:T(8,128)(2,1)S(1)}, u32[]{:S(2)}, u32[]{:S(2)}) collective-permute-start(f16[2,64,256]{2,1,0:T(8,128)(2,1)S(1)} %get-tuple-element.61), channel_id=1, source_target_pairs={{0,4},{1,5},{2,6},{3,7},{4,0},{5,1},{6,2},{7,3},{8,12},{9,13},{10,... | collective-permute-start | bytes 196616 | tf_op jit(solution)/shard_map/ppermute | solution.py:143
  219.1 6.8 %collective-permute-start.13 = (f16[2,64,256]{2,1,0:T(8,128)(2,1)S(1)}, f16[2,64,256]{2,1,0:T(8,128)(2,1)S(1)}, u32[]{:S(2)}, u32[]{:S(2)}) collective-permute-start(f16[2,64,256]{2,1,0:T(8,128)(2,1)S(1)} %get-tuple-element.60), channel_id=1, source_target_pairs={{0,2},{1,3},{2,0},{3,1},{4,6},{5,7},{6,4},{7,5},{8,10},{9,11},{10,... | collective-permute-start | bytes 196616 | tf_op jit(solution)/shard_map/ppermute | solution.py:143
  220.3 7.4 %collective-permute-start.7 = (f16[2,64,256]{2,1,0:T(8,128)(2,1)S(1)}, f16[2,64,256]{2,1,0:T(8,128)(2,1)S(1)}, u32[]{:S(2)}, u32[]{:S(2)}) collective-permute-start(f16[2,64,256]{2,1,0:T(8,128)(2,1)S(1)} %get-tuple-element.59), channel_id=1, source_target_pairs={{0,6},{1,7},{2,4},{3,5},{4,2},{5,3},{6,0},{7,1},{8,14},{9,15},{10,... | collective-permute-start | bytes 196616 | tf_op jit(solution)/shard_map/ppermute | solution.py:143
  223.7 5.2 %collective-permute-start.6 = (f16[2,64,256]{2,1,0:T(8,128)(2,1)S(1)}, f16[2,64,256]{2,1,0:T(8,128)(2,1)S(1)}, u32[]{:S(2)}, u32[]{:S(2)}) collective-permute-start(f16[2,64,256]{2,1,0:T(8,128)(2,1)S(1)} %get-tuple-element.58), channel_id=1, source_target_pairs={{0,4},{1,5},{2,6},{3,7},{4,0},{5,1},{6,2},{7,3},{8,12},{9,13},{10,... | collective-permute-start | bytes 196616 | tf_op jit(solution)/shard_map/ppermute | solution.py:143
  223.7 5.2 %collective-permute-start.5 = (f16[2,64,256]{2,1,0:T(8,128)(2,1)S(1)}, f16[2,64,256]{2,1,0:T(8,128)(2,1)S(1)}, u32[]{:S(2)}, u32[]{:S(2)}) collective-permute-start(f16[2,64,256]{2,1,0:T(8,128)(2,1)S(1)} %get-tuple-element.57), channel_id=1, source_target_pairs={{0,2},{1,3},{2,0},{3,1},{4,6},{5,7},{6,4},{7,5},{8,10},{9,11},{10,... | collective-permute-start | bytes 196616 | tf_op jit(solution)/shard_map/ppermute | solution.py:143
  226.1 4.4 %collective-permute-start.21 = (f16[64,128]{1,0:T(8,128)(2,1)S(1)}, f16[64,128]{1,0:T(8,128)(2,1)S(1)}, u32[]{:S(2)}, u32[]{:S(2)}) collective-permute-start(f16[64,128]{1,0:T(8,128)(2,1)S(1)} %get-tuple-element.84), channel_id=1, source_target_pairs={{0,24},{1,25},{2,26},{3,27},{4,28},{5,29},{6,30},{7,31},{8,16},{9,... | collective-permute-start | bytes 49160 | tf_op jit(solution)/shard_map/ppermute | solution.py:143
  226.2 4.9 %collective-permute-start.20 = (f16[64,128]{1,0:T(8,128)(2,1)S(1)}, f16[64,128]{1,0:T(8,128)(2,1)S(1)}, u32[]{:S(2)}, u32[]{:S(2)}) collective-permute-start(f16[64,128]{1,0:T(8,128)(2,1)S(1)} %get-tuple-element.85), channel_id=1, source_target_pairs={{0,16},{1,17},{2,18},{3,19},{4,20},{5,21},{6,22},{7,23},{8,24},{9,... | collective-permute-start | bytes 49160 | tf_op jit(solution)/shard_map/ppermute | solution.py:143
  227.7 3.4 %collective-permute-start.19 = (f16[64,128]{1,0:T(8,128)(2,1)S(1)}, f16[64,128]{1,0:T(8,128)(2,1)S(1)}, u32[]{:S(2)}, u32[]{:S(2)}) collective-permute-start(f16[64,128]{1,0:T(8,128)(2,1)S(1)} %get-tuple-element.86), channel_id=1, source_target_pairs={{0,8},{1,9},{2,10},{3,11},{4,12},{5,13},{6,14},{7,15},{8,0},{9,1},... | collective-permute-start | bytes 49160 | tf_op jit(solution)/shard_map/ppermute | solution.py:143
  229.1 33.6 %collective-permute-start.18 = (f16[64,128]{1,0:T(8,128)(2,1)S(1)}, f16[64,128]{1,0:T(8,128)(2,1)S(1)}, u32[]{:S(2)}, u32[]{:S(2)}) collective-permute-start(f16[64,128]{1,0:T(8,128)(2,1)S(1)} %get-tuple-element.80), channel_id=1, source_target_pairs={{0,24},{1,25},{2,26},{3,27},{4,28},{5,29},{6,30},{7,31},{8,16},{9,... | collective-permute-start | bytes 49160 | tf_op jit(solution)/shard_map/ppermute | solution.py:143
  229.4 33.4 %collective-permute-start.17 = (f16[64,128]{1,0:T(8,128)(2,1)S(1)}, f16[64,128]{1,0:T(8,128)(2,1)S(1)}, u32[]{:S(2)}, u32[]{:S(2)}) collective-permute-start(f16[64,128]{1,0:T(8,128)(2,1)S(1)} %get-tuple-element.81), channel_id=1, source_target_pairs={{0,16},{1,17},{2,18},{3,19},{4,20},{5,21},{6,22},{7,23},{8,24},{9,... | collective-permute-start | bytes 49160 | tf_op jit(solution)/shard_map/ppermute | solution.py:143
  230.5 32.2 %collective-permute-start.16 = (f16[64,128]{1,0:T(8,128)(2,1)S(1)}, f16[64,128]{1,0:T(8,128)(2,1)S(1)}, u32[]{:S(2)}, u32[]{:S(2)}) collective-permute-start(f16[64,128]{1,0:T(8,128)(2,1)S(1)} %get-tuple-element.82), channel_id=1, source_target_pairs={{0,8},{1,9},{2,10},{3,11},{4,12},{5,13},{6,14},{7,15},{8,0},{9,1},... | collective-permute-start | bytes 49160 | tf_op jit(solution)/shard_map/ppermute | solution.py:143
  294.2 6.3 %copy-start.7 = (f32[2,4,64,256]{3,2,1,0:T(8,128)S(1)}, f32[2,4,64,256]{3,2,1,0:T(8,128)}, u32[]{:S(2)}) copy-start(f32[2,4,64,256]{3,2,1,0:T(8,128)} %param.13) | copy-start | bytes 1572868
  294.2 6.3 %copy-start.10 = (f32[2,4,64,256]{3,2,1,0:T(8,128)S(1)}, f32[2,4,64,256]{3,2,1,0:T(8,128)}, u32[]{:S(2)}) copy-start(f32[2,4,64,256]{3,2,1,0:T(8,128)} %custom-call) | copy-start | bytes 1572868
  (4 other events, 3.5 us)
Sparse Core Ops, SparseCore 0:
  19.0 64.7 all-gather.5
  86.8 60.6 all-gather.7

commit v3 on v2

v3 whole, which is shorter than its diff:
```python
import functools
import math

import jax
import jax.numpy as jnp
from jax import lax
from jax.experimental import pallas as pl
from jax.experimental.pallas import tpu as pltpu
from jax.sharding import PartitionSpec as P

AXES = ("node", "cores")


def ladder_kernel(dims, mask_ref, tasks_ref, owner_ref, fitted_ref, *refs):
    nodes, cores, slots_here, rows, tile, aux, slots, side = dims
    first_refs, second_refs, refs = refs[:nodes], refs[nodes:nodes + 4], refs[nodes + 4:]
    keep_ref, send_ref, left_buf, right_buf, half_buf, tile_buf, total, work, slot_of, load_sems, store_sems = refs
    task_count = tasks_ref.shape[0]
    node_index = lax.axis_index("node")
    core_index = lax.axis_index("cores")
    block = node_index * cores + core_index

    def invert(s, carry):
        slot_of[owner_ref[s]] = s
        return carry

    lax.fori_loop(0, slots, invert, 0)

    def indices(t):
        out_tile = tasks_ref[t, 0]
        in_tile = tasks_ref[t, 1]
        a, b = out_tile // side, out_tile % side
        c, d = in_tile // side, in_tile % side
        return a, b, a * side + c, b * side + d, in_tile

    def enlist(t, count):
        _, _, left, right, _ = indices(t)
        work[count] = t
        return count + mask_ref[left, block] * mask_ref[right, block]

    active = lax.fori_loop(0, task_count, enlist, jnp.int32(0))

    def start_loads(i, slot):
        _, _, left, right, in_tile = indices(work[i])
        place = slot_of[in_tile]
        inside = place % slots_here
        apart = (place // slots_here) ^ core_index
        low, far = apart % 2, apart // 2

        def fetch(source, p, other):
            strip = pl.ds(pl.multiple_of((node_index ^ other) * rows, rows), rows)
            pltpu.make_async_copy(source, tile_buf.at[slot, p, strip, :], load_sems.at[slot, 2]).start()

        for other in range(nodes):
            fetch(first_refs[other].at[low, far, inside], 0, other)
        for x in range(2):

            @pl.when(low == x)
            def _():
                for other in range(nodes):
                    fetch(second_refs[(other % 2) * 2 + x].at[other // 2, far, inside], 1, other)

        pltpu.make_async_copy(fitted_ref.at[left], left_buf.at[slot], load_sems.at[slot, 0]).start()
        for q in range(aux):
            pltpu.make_async_copy(
                fitted_ref.at[right, q], right_buf.at[slot, :, pl.ds(q * tile, tile)], load_sems.at[slot, 1]
            ).start()

    def wait_loads(slot):
        for k, buf in enumerate((left_buf, right_buf, tile_buf)):
            pltpu.make_async_copy(buf.at[slot], buf.at[slot], load_sems.at[slot, k]).wait()

    @pl.when(active > 0)
    def _():
        start_loads(0, 0)

    @pl.loop(0, slots)
    def _(s):
        total[s] = jnp.zeros(total.shape[1:], jnp.float32)

    def contract(first, second):
        return lax.dot_general(first, second, (((1,), (1,)), ((), ())), preferred_element_type=jnp.float32)

    @pl.loop(0, active)
    def _(i):
        slot = i % 2

        @pl.when(i + 1 < active)
        def _():
            start_loads(i + 1, 1 - slot)

        wait_loads(slot)
        a, b, _, _, _ = indices(work[i])
        straight = slot_of[a * side + b]
        crossed = slot_of[b * side + a]
        left_all = left_buf[slot].reshape(aux * tile, tile)
        for p in range(2):
            half = jnp.dot(left_all, tile_buf[slot, p], preferred_element_type=jnp.float32).astype(jnp.bfloat16)
            for q in range(aux):
                half_buf[p, :, q * tile:(q + 1) * tile] = half[q * tile:(q + 1) * tile]
        shape = total.shape[1:]
        total[straight] += contract(half_buf[0], right_buf[slot]).reshape(shape)
        total[crossed] += contract(right_buf[slot], half_buf[1]).reshape(shape)

    mine = node_index % 2
    stores = [
        pltpu.make_async_copy(total.at[:, :, mine], keep_ref, store_sems.at[0]),
        pltpu.make_async_copy(total.at[:, :, 1 - mine], send_ref, store_sems.at[1]),
    ]
    for copy in stores:
        copy.start()
    for copy in stores:
        copy.wait()


def ladder_terms(mask, tasks, owner_map, fitted, first, second, nodes, cores):
    tile_pairs, aux, tile, _ = fitted.shape
    slots_here, rows = first[0].shape[2:4]
    side = math.isqrt(tile_pairs)
    dims = (nodes, cores, slots_here, rows, tile, aux, tile_pairs, side)
    smem = pl.BlockSpec(memory_space=pltpu.SMEM)
    hbm = pl.BlockSpec(memory_space=pl.ANY)
    part = jax.ShapeDtypeStruct((tile_pairs, nodes // 2, rows, tile), jnp.float32)
    return pl.pallas_call(
        functools.partial(ladder_kernel, dims),
        out_shape=(part, part),
        in_specs=[smem, smem, smem] + [hbm] * (1 + len(first) + len(second)),
        out_specs=(hbm, hbm),
        scratch_shapes=[
            pltpu.VMEM((2, aux, tile, tile), jnp.bfloat16),
            pltpu.VMEM((2, tile, aux * tile), jnp.bfloat16),
            pltpu.VMEM((2, tile, aux * tile), jnp.bfloat16),
            pltpu.VMEM((2, 2, tile, tile), jnp.bfloat16),
            pltpu.VMEM((tile_pairs, nodes // 2, 2, rows, tile), jnp.float32),
            pltpu.SMEM((tasks.shape[0] + 1,), jnp.int32),
            pltpu.SMEM((tile_pairs,), jnp.int32),
            pltpu.SemaphoreType.DMA((2, 3)),
            pltpu.SemaphoreType.DMA((2,)),
        ],
        compiler_params=pltpu.CompilerParams(vmem_limit_bytes=32 * 1024 * 1024),
        cost_estimate=pl.CostEstimate(flops=20 * 10**9, bytes_accessed=30 * 2**20, transcendentals=0),
        name="ladder",
    )(mask, tasks, owner_map, fitted, *first, *second)


def swap(array, mask, total):
    return lax.ppermute(array, AXES, [(i, i ^ mask) for i in range(total)])


def pick(array, index, axis):
    return lax.dynamic_index_in_dim(array, index, axis, keepdims=False)


def halve(value, index, axis, mask, total):
    shape = value.shape
    split = value.reshape(shape[:axis] + (shape[axis] // 2, 2) + shape[axis + 1:])
    other = swap(pick(split, 1 - index, axis + 1), mask, total)
    own = pick(split, index, axis + 1)
    return (own.astype(jnp.float32) + other.astype(jnp.float32)).astype(value.dtype)


def reduce_blocks(keep, send, nodes, cores, scale):
    total = nodes * cores
    node_index = lax.axis_index("node")
    core_index = lax.axis_index("cores")
    slots, inner, rows, tile = keep.shape
    got = swap(send, cores, total)
    part = ((keep + got) * scale).astype(jnp.float16).reshape(cores, slots // cores, inner, rows, tile)

    def over_inner(value):
        mask, index = 2 * cores, node_index // 2
        while value.shape[2] > 1:
            value = halve(value, index % 2, 2, mask, total)
            mask, index = mask * 2, index // 2
        return value

    def over_low(value):
        return halve(value, core_index % 2, 0, 1, total)

    upper = over_low(over_inner(part[:, :, :, :rows // 2]))
    lower = over_inner(over_low(part[:, :, :, rows // 2:]))
    part = jnp.concatenate([upper, lower], axis=3)[:, :, 0]
    at = core_index // 2
    mine = pick(part, at, 0).astype(jnp.float32)
    for step in range(1, part.shape[0]):
        mine = mine + swap(pick(part, at ^ step, 0), 2 * step, total).astype(jnp.float32)
    return mine * (0.5 / scale)


def pair_groups(partner_ref, pairs):
    count = jnp.int32(0)
    chosen = [jnp.int32(0)] * (pairs // 2)
    for p in range(pairs):
        is_rep = p < partner_ref[p]
        chosen = [jnp.where(is_rep & (count == g), p, old) for g, old in enumerate(chosen)]
        count = count + is_rep.astype(jnp.int32)
    return [(p, partner_ref[p]) for p in chosen]


def lower_kernel(partner_ref, amps_ref, *out_refs):
    for g, both in enumerate(pair_groups(partner_ref, amps_ref.shape[1])):
        for role, p in enumerate(both):
            out_refs[2 * g + role][...] = amps_ref[:, p].astype(jnp.bfloat16)


def lower(partner, amplitudes):
    slots_here, pairs, rows, tile = amplitudes.shape
    vmem = pl.BlockSpec(memory_space=pltpu.VMEM)
    return pl.pallas_call(
        lower_kernel,
        out_shape=(jax.ShapeDtypeStruct((slots_here, rows, tile), jnp.bfloat16),) * pairs,
        in_specs=[pl.BlockSpec(memory_space=pltpu.SMEM), vmem],
        out_specs=(vmem,) * pairs,
        name="lower",
    )(partner, amplitudes)


def spread_far(part, cores, total):
    return jnp.stack([part] + [swap(part, 2 * step, total) for step in range(1, cores // 2)])


def spread_first(part, nodes, cores):
    total = nodes * cores
    part = spread_far(part, cores, total)
    pieces = {0: jnp.stack([part, swap(part, 1, total)])}
    bit = nodes // 2
    while bit:
        pieces.update({other | bit: swap(piece, bit * cores, total) for other, piece in pieces.items()})
        bit //= 2
    return [pieces[other] for other in range(nodes)]


def spread_second(part, nodes, cores):
    total = nodes * cores
    pieces = {0: spread_far(part, cores, total)}
    bit = nodes // 2
    while bit > 1:
        pieces.update({other | bit: swap(piece, bit * cores, total) for other, piece in pieces.items()})
        bit //= 2
    near = jnp.stack([pieces[2 * upper] for upper in range(nodes // 2)])
    far = swap(near, 1, total)
    return [near, far, swap(near, cores, total), swap(far, cores, total)]


def turn_blocks(mine, far_first, nodes, cores, scale):
    total = nodes * cores
    slots_here, rows, tile = mine.shape
    node_index = lax.axis_index("node")
    turned = (mine * scale).astype(jnp.float16).reshape(slots_here * rows, tile).T
    turned = turned.reshape(nodes, rows, slots_here * rows)
    pieces = [pick(turned, node_index, 0)]
    pieces += [swap(pick(turned, node_index ^ step, 0), step * cores, total) for step in range(1, nodes)]
    pieces = jnp.stack(pieces)
    block = jnp.stack([pick(pieces, node_index ^ n, 0) for n in range(nodes)])
    block = block.reshape(nodes, rows, slots_here, rows).transpose(2, 1, 0, 3).reshape(slots_here, rows, tile)
    if far_first:
        near = spread_far(block, cores, total)
        every = jnp.stack([near, swap(near, 1, total)], axis=1)
    else:
        every = spread_far(jnp.stack([block, swap(block, 1, total)]), cores, total)
    return every.reshape(cores, slots_here, rows, tile).astype(jnp.float32) * (1.0 / scale)


def update_kernel(side, owner_ref, partner_ref, pair_ref, energy_ref, column_ref, amps_ref, *refs):
    slots_here, pairs, rows, tile = amps_ref.shape
    groups = pairs // 2
    straight, crossed, out_ref, slot_of = refs[:groups], refs[groups:2 * groups], refs[-2], refs[-1]
    node_index = lax.axis_index("node")
    core_index = lax.axis_index("cores")

    def invert(s, carry):
        slot_of[owner_ref[s]] = s
        return carry

    lax.fori_loop(0, owner_ref.shape[0], invert, 0)
    for j in range(slots_here):
        mine = owner_ref[core_index * slots_here + j]
        row_tile, col_tile = mine // side, mine % side
        place = slot_of[col_tile * side + row_tile]
        apart, inside = (place // slots_here) ^ core_index, place % slots_here
        row_energy = energy_ref[pl.ds(pl.multiple_of(row_tile * tile + node_index * rows, 8), rows), :]
        col_energy = column_ref[pl.ds(col_tile, 1), :]
        for g, (rep, twin) in enumerate(pair_groups(partner_ref, pairs)):
            for p, value in ((rep, straight[g][j]), (twin, crossed[g][apart, inside])):
                denominator = (pair_ref[p] - row_energy) - col_energy
                out_ref[j, p] = amps_ref[j, p] + value / denominator


def update(owner_map, partner, pair_energy, virt_energy, amplitudes, straight, crossed):
    tile = amplitudes.shape[3]
    smem = pl.BlockSpec(memory_space=pltpu.SMEM)
    vmem = pl.BlockSpec(memory_space=pltpu.VMEM)
    return pl.pallas_call(
        functools.partial(update_kernel, math.isqrt(owner_map.shape[0])),
        out_shape=jax.ShapeDtypeStruct(amplitudes.shape, jnp.float32),
        in_specs=[smem] * 3 + [vmem] * (3 + len(straight) + len(crossed)),
        out_specs=vmem,
        scratch_shapes=[pltpu.SMEM(owner_map.shape, jnp.int32)],
        compiler_params=pltpu.CompilerParams(vmem_limit_bytes=32 * 1024 * 1024),
        name="update",
    )(
        owner_map, partner, pair_energy, virt_energy.reshape(-1, 1), virt_energy.reshape(-1, tile),
        amplitudes, *straight, *crossed,
    )


def body(nodes, cores, fitted, fit_mask, tasks, owner_map, partner, amplitudes, pair_energy, virt_energy):
    scale = 2.0 ** -9
    parts = lower(partner, amplitudes)
    groups = len(parts) // 2
    first = [spread_first(parts[2 * g], nodes, cores) for g in range(groups)]
    second = [spread_second(parts[2 * g + 1], nodes, cores) for g in range(groups)]
    straight, crossed = [], []
    for g in range(groups):
        keep, send = ladder_terms(fit_mask, tasks, owner_map, fitted, first[g], second[g], nodes, cores)
        mine = reduce_blocks(keep, send, nodes, cores, scale)
        straight.append(mine)
        crossed.append(turn_blocks(mine, g == 0, nodes, cores, scale))
    return update(owner_map, partner, pair_energy, virt_energy, amplitudes, straight, crossed)


def solution(mesh):
    placed = (P(None, AXES, None, None), P(), P(), P(), P(), P("cores", None, "node", None), P(), P())
    return jax.shard_map(
        functools.partial(body, mesh.shape["node"], mesh.shape["cores"]),
        mesh=mesh, in_specs=placed, out_specs=P("cores", None, "node", None), check_vma=False,
    )
```

time: 311 us -> 199 us (0.64)
  waiting for transfers between devices: 115 us -> 46.1 us
  blocking collectives: 62.6 us -> 0 us
  starting transfers between devices: 36.8 us -> 80.2 us
  between operations: 34.5 us -> 0.76 us
  Pallas kernels: 25.9 us -> 47.4 us
  other arithmetic: 18 us -> 9.26 us
    all_gather x2 -> x0, waiting for transfers between devices: 102 us -> none  [body(): gathered.append(lax.all_gather(lowered, AXES, axis=0, tiled=False))]
    all_gather x2 -> x0, blocking collectives: 62.6 us -> none  [turn_blocks(): every = lax.all_gather(pieces, 'cores', axis=0, tiled=False)]
    ppermute x22 -> x58, starting transfers between devices: 36.7 us -> 80.2 us  [swap(): return lax.ppermute(array, AXES, [(i, i ^ mask) for i in range(total)])]
    ppermute x22 -> x58, waiting for transfers between devices: 13.1 us -> 46.1 us  [swap(): return lax.ppermute(array, AXES, [(i, i ^ mask) for i in range(total)])]
    pallas_call x2, Pallas kernels: 25.9 us -> 43.9 us  [ladder_terms(): pl.pallas_call(functools.partial(ladder_kernel, dims), out_shape=(part, p...]
    pallas_call x0 -> x2, Pallas kernels: none -> 3.47 us  [the longest x1 1.78 us: lower(): pl.pallas_call(lower_kernel, out_shape=(jax.ShapeDtypeStruct((slots_here,...]
    another operation x8 -> x14, other arithmetic: 6.85 us -> 3.94 us  [the longest x4 1.88 us: spread_second(): near = jnp.stack([pieces[2 * upper] for upper in range(nodes // 2)])]
    unnamed x27 -> x45, local copies, waits for them, and re-layouts: 8.79 us -> 11.6 us
  transfers between devices with their start and end apart: 24 -> 58, of which waited for: 8 -> 17; matrix products, arithmetic and copies ran while one was open for 5% -> 5% of each run, Pallas kernels for 8% -> 22%
where the time goes in v3:
time: 199 us; the launch traced here: 198 us
  starting transfers between devices  80.2 us (40%)
  Pallas kernels  47.4 us (24%)
  waiting for transfers between devices  46.1 us (23%)
  local copies, waits for them, and re-layouts  14.6 us (7%)
  other arithmetic  9.26 us (5%)
    ppermute x58, starting transfers between devices, swap(): return lax.ppermute(array, AXES, [(i, i ^ mask) for i in range(total)])  80.2 us
    ppermute x58, waiting for transfers between devices, swap(): return lax.ppermute(array, AXES, [(i, i ^ mask) for i in range(total)])  46.1 us
    pallas_call x2, Pallas kernels, ladder_terms(): pl.pallas_call(functools.partial(ladder_kernel, dims), out_shape=(part, p...  43.9 us
    unnamed x45, local copies, waits for them, and re-layouts  11.6 us
    convert_element_type x2, other arithmetic, reduce_blocks(): ((keep + got) * scale).astype(jnp.float16)  4.19 us
  transfers between devices with their start and end apart: 58, of which 17 were waited for; matrix products, arithmetic and copies ran while one was open for 5% of the time, Pallas kernels for 22%

profile of v3, /device:TPU:0, one launch (start us, length us, event | category | flops | bytes accessed | tf_op | source)
XLA Modules:
  0.0 198.2 jit_solution(12067014702037346851)
XLA Ops:
  0.0 1.8 lower.1
  1.8 3.1 %collective-permute-start.22 = (bf16[2,64,256]{2,1,0:T(8,128)(2,1)}, bf16[2,64,256]{2,1,0:T(8,128)(2,1)S(1)}, u32[]{:S(2)}, u32[]{:S(2)}) collective-permute-start(bf16[2,64,256]{2,1,0:T(8,128)(2,1)} %get-tuple-element.17), channel_id=1, source_target_pairs={{0,2},{1,3},{2,0},{3,1},{4,6},{5,7},{6,4},{7,5},{8,10},{9,11},{10,... | collective-permute-start | bytes 196616 | tf_op jit(solution)/shard_map/ppermute | solution.py:147
  4.8 2.6 %collective-permute-start.23 = (bf16[2,64,256]{2,1,0:T(8,128)(2,1)}, bf16[2,64,256]{2,1,0:T(8,128)(2,1)S(1)}, u32[]{:S(2)}, u32[]{:S(2)}) collective-permute-start(bf16[2,64,256]{2,1,0:T(8,128)(2,1)} %get-tuple-element.17), channel_id=1, source_target_pairs={{0,4},{1,5},{2,6},{3,7},{4,0},{5,1},{6,2},{7,3},{8,12},{9,13},{10,... | collective-permute-start | bytes 196616 | tf_op jit(solution)/shard_map/ppermute | solution.py:147
  8.3 3.5 %collective-permute-start.30 = (bf16[2,64,256]{2,1,0:T(8,128)(2,1)}, bf16[2,64,256]{2,1,0:T(8,128)(2,1)S(1)}, u32[]{:S(2)}, u32[]{:S(2)}) collective-permute-start(bf16[2,64,256]{2,1,0:T(8,128)(2,1)} %get-tuple-element.18), channel_id=1, source_target_pairs={{0,4},{1,5},{2,6},{3,7},{4,0},{5,1},{6,2},{7,3},{8,12},{9,13},{10,... | collective-permute-start | bytes 196616 | tf_op jit(solution)/shard_map/ppermute | solution.py:147
  12.4 1.8 collective-permute-done.24
  16.7 2.0 %collective-permute-done.30 = bf16[2,64,256]{2,1,0:T(8,128)(2,1)S(1)} collective-permute-done((bf16[2,64,256]{2,1,0:T(8,128)(2,1)}, bf16[2,64,256]{2,1,0:T(8,128)(2,1)S(1)}, u32[]{:S(2)}, u32[]{:S(2)}) %collective-permute-start.30) | collective-permute-done | bytes 65568 | tf_op jit(solution)/shard_map/ppermute | solution.py:147
  21.1 2.5 %collective-permute-start.9 = (bf16[2,64,256]{2,1,0:T(8,128)(2,1)}, bf16[2,64,256]{2,1,0:T(8,128)(2,1)S(1)}, u32[]{:S(2)}, u32[]{:S(2)}) collective-permute-start(bf16[2,64,256]{2,1,0:T(8,128)(2,1)} %get-tuple-element.14), channel_id=1, source_target_pairs={{0,6},{1,7},{2,4},{3,5},{4,2},{5,3},{6,0},{7,1},{8,14},{9,15},{10,... | collective-permute-start | bytes 196616 | tf_op jit(solution)/shard_map/ppermute | solution.py:147
  26.3 2.7 %collective-permute-start.1 = (bf16[2,64,256]{2,1,0:T(8,128)(2,1)S(1)}, bf16[2,64,256]{2,1,0:T(8,128)(2,1)S(1)}, u32[]{:S(2)}, u32[]{:S(2)}) collective-permute-start(bf16[2,64,256]{2,1,0:T(8,128)(2,1)S(1)} %copy-done.17), channel_id=1, source_target_pairs={{0,4},{1,5},{2,6},{3,7},{4,0},{5,1},{6,2},{7,3},{8,12},{9,13},{10,... | collective-permute-start | bytes 196616 | tf_op jit(solution)/shard_map/ppermute | solution.py:147
  36.7 11.0 %collective-permute-done.10 = bf16[4,2,64,256]{3,2,1,0:T(8,128)(2,1)S(1)} collective-permute-done((bf16[4,2,64,256]{3,2,1,0:T(8,128)(2,1)S(1)}, bf16[4,2,64,256]{3,2,1,0:T(8,128)(2,1)S(1)}, u32[]{:S(2)}, u32[]{:S(2)}) %collective-permute-start.10) | collective-permute-done | bytes 262176 | tf_op jit(solution)/shard_map/ppermute | solution.py:147
  48.5 4.6 %collective-permute-done.3 = bf16[4,2,64,256]{3,2,1,0:T(8,128)(2,1)S(1)} collective-permute-done((bf16[4,2,64,256]{3,2,1,0:T(8,128)(2,1)S(1)}, bf16[4,2,64,256]{3,2,1,0:T(8,128)(2,1)S(1)}, u32[]{:S(2)}, u32[]{:S(2)}) %collective-permute-start.3) | collective-permute-done | bytes 262176 | tf_op jit(solution)/shard_map/ppermute | solution.py:147
  59.1 8.0 %collective-permute-done.11.refs_5_ = bf16[2,4,2,64,256]{4,3,2,1,0:T(8,128)(2,1)} collective-permute-done((bf16[2,4,2,64,256]{4,3,2,1,0:T(8,128)(2,1)}, bf16[2,4,2,64,256]{4,3,2,1,0:T(8,128)(2,1)}, u32[]{:S(2)}, u32[]{:S(2)}) %collective-permute-start.11) | collective-permute-done | bytes 524320 | tf_op jit(solution)/shard_map/ppermute | solution.py:147
  67.0 1.8 collective-permute-done.5.refs_2_
  75.3 22.4 %ladder.3 = (f32[16,2,64,256]{3,2,1,0:T(8,128)S(1)}, f32[16,2,64,256]{3,2,1,0:T(8,128)}) custom-call(s32[16,32]{1,0:T(8,128)S(1)} %copy-done.16, s32[16,2]{1,0:T(8,128)S(1)} %copy.26.tasks_ref, s32[16]{0:T(128)S(1)} %copy-done.4, bf16[16,8,256,256]{3,2,1,0:T(8,128)(2,1)} %fitted_ref.3, bf16[2,4,2,64,256]{4,3,2,1,0:T(8,128)(2,1)S(1)} %pad_maximum_fusion.2.refs_0_, ...), custom_call_target="tpu_custom_call" | custom-call | flops 20000000000 | bytes 31457280 | tf_op jit(solution)/shard_map/ladder/pallas_call | solution.py:124
  97.9 21.5 %ladder.2 = (f32[16,2,64,256]{3,2,1,0:T(8,128)S(1)}, f32[16,2,64,256]{3,2,1,0:T(8,128)}) custom-call(s32[16,32]{1,0:T(8,128)S(1)} %copy-done.16, s32[16,2]{1,0:T(8,128)S(1)} %copy.26.tasks_ref, s32[16]{0:T(128)S(1)} %copy-done.4, bf16[16,8,256,256]{3,2,1,0:T(8,128)(2,1)} %fitted_ref.3, bf16[2,4,2,64,256]{4,3,2,1,0:T(8,128)(2,1)} %pad_maximum_fusion.refs_0_, ...), custom_call_target="tpu_custom_call" | custom-call | flops 20000000000 | bytes 31457280 | tf_op jit(solution)/shard_map/ladder/pallas_call | solution.py:124
  120.8 2.1 %multiply_convert_fusion = f16[16,2,64,256]{3,2,1,0:T(8,128)(2,1)S(1)} fusion(f32[16,2,64,256]{3,2,1,0:T(8,128)S(1)} %get-tuple-element.19, f32[16,2,64,256]{3,2,1,0:T(8,128)} %collective-permute-done.36), kind=kLoop, calls=%fused_computation | loop fusion | flops 1572864 | bytes 5242880 | tf_op jit(solution)/shard_map/convert_element_type | solution.py:168
  123.2 2.1 %collective-permute-done.14 = f32[16,2,64,256]{3,2,1,0:T(8,128)} collective-permute-done((f32[16,2,64,256]{3,2,1,0:T(8,128)}, f32[16,2,64,256]{3,2,1,0:T(8,128)}, u32[]{:S(2)}, u32[]{:S(2)}) %collective-permute-start.14) | collective-permute-done | bytes 2097184 | tf_op jit(solution)/shard_map/ppermute | solution.py:147
  125.3 2.1 %multiply_convert_fusion.1 = f16[16,2,64,256]{3,2,1,0:T(8,128)(2,1)S(1)} fusion(f32[16,2,64,256]{3,2,1,0:T(8,128)S(1)} %copy-done.2, f32[16,2,64,256]{3,2,1,0:T(8,128)} %collective-permute-done.14), kind=kLoop, calls=%fused_computation.1 | loop fusion | flops 1572864 | bytes 5242880 | tf_op jit(solution)/shard_map/convert_element_type | solution.py:168
  128.3 7.4 %collective-permute-start.37 = (f16[8,2,1,32,256]{4,3,1,0,2:T(8,128)(2,1)S(1)}, f16[8,2,1,32,256]{4,3,1,0,2:T(8,128)(2,1)S(1)}, u32[]{:S(2)}, u32[]{:S(2)}) collective-permute-start(f16[8,2,1,32,256]{4,3,1,0,2:T(8,128)(2,1)S(1)} %dynamic-slice_bitcast_fusion), channel_id=1, source_target_pairs={{0,16},{1,17},{2,18},{3,19},{4,20},{5,21},{6,22},{7,23},{8,24},{9,... | collective-permute-start | bytes 786440 | tf_op jit(solution)/shard_map/ppermute | solution.py:147
  136.6 6.2 %collective-permute-start.40 = (f16[4,2,1,32,256]{4,3,1,2,0:T(8,128)(2,1)S(1)}, f16[4,2,1,32,256]{4,3,1,2,0:T(8,128)(2,1)S(1)}, u32[]{:S(2)}, u32[]{:S(2)}) collective-permute-start(f16[4,2,1,32,256]{4,3,1,2,0:T(8,128)(2,1)S(1)} %constant_dynamic-slice_fusion.10), channel_id=1, source_target_pairs={{0,16},{1,17},{2,18},{3,19},{4,20},{5,21},{6,22},{7,23},{8,24},{9,... | collective-permute-start | bytes 393224 | tf_op jit(solution)/shard_map/ppermute | solution.py:147
  143.0 2.1 %collective-permute-start.38 = (f16[4,2,1,32,256]{4,3,1,2,0:T(8,128)(2,1)S(1)}, f16[4,2,1,32,256]{4,3,1,2,0:T(8,128)(2,1)S(1)}, u32[]{:S(2)}, u32[]{:S(2)}) collective-permute-start(f16[4,2,1,32,256]{4,3,1,2,0:T(8,128)(2,1)S(1)} %dynamic-slice_bitcast_fusion.2), channel_id=1, source_target_pairs={{0,1},{1,0},{2,3},{3,2},{4,5},{5,4},{6,7},{7,6},{8,9},{9,8},{10,11... | collective-permute-start | bytes 393224 | tf_op jit(solution)/shard_map/ppermute | solution.py:147
  145.3 3.2 %collective-permute-start.18 = (f16[4,2,1,32,256]{4,3,1,2,0:T(8,128)(2,1)S(1)}, f16[4,2,1,32,256]{4,3,1,2,0:T(8,128)(2,1)S(1)}, u32[]{:S(2)}, u32[]{:S(2)}) collective-permute-start(f16[4,2,1,32,256]{4,3,1,2,0:T(8,128)(2,1)S(1)} %constant_dynamic-slice_fusion.13), channel_id=1, source_target_pairs={{0,16},{1,17},{2,18},{3,19},{4,20},{5,21},{6,22},{7,23},{8,24},{9,... | collective-permute-start | bytes 393224 | tf_op jit(solution)/shard_map/ppermute | solution.py:147
  148.7 2.1 %collective-permute-start.16 = (f16[4,2,1,32,256]{4,3,1,2,0:T(8,128)(2,1)S(1)}, f16[4,2,1,32,256]{4,3,1,2,0:T(8,128)(2,1)S(1)}, u32[]{:S(2)}, u32[]{:S(2)}) collective-permute-start(f16[4,2,1,32,256]{4,3,1,2,0:T(8,128)(2,1)S(1)} %dynamic-slice_bitcast_fusion.3), channel_id=1, source_target_pairs={{0,1},{1,0},{2,3},{3,2},{4,5},{5,4},{6,7},{7,6},{8,9},{9,8},{10,11... | collective-permute-start | bytes 393224 | tf_op jit(solution)/shard_map/ppermute | solution.py:147
  151.5 8.8 %collective-permute-start.42 = (f16[2,64,256]{2,1,0:T(8,128)(2,1)S(1)}, f16[2,64,256]{2,1,0:T(8,128)(2,1)S(1)}, u32[]{:S(2)}, u32[]{:S(2)}) collective-permute-start(f16[2,64,256]{2,1,0:T(8,128)(2,1)S(1)} %get-tuple-element.36), channel_id=1, source_target_pairs={{0,4},{1,5},{2,6},{3,7},{4,0},{5,1},{6,2},{7,3},{8,12},{9,13},{10,... | collective-permute-start | bytes 196616 | tf_op jit(solution)/shard_map/ppermute | solution.py:147
  161.1 3.8 %collective-permute-start.20 = (f16[2,64,256]{2,1,0:T(8,128)(2,1)S(1)}, f16[2,64,256]{2,1,0:T(8,128)(2,1)S(1)}, u32[]{:S(2)}, u32[]{:S(2)}) collective-permute-start(f16[2,64,256]{2,1,0:T(8,128)(2,1)S(1)} %get-tuple-element.43), channel_id=1, source_target_pairs={{0,4},{1,5},{2,6},{3,7},{4,0},{5,1},{6,2},{7,3},{8,12},{9,13},{10,... | collective-permute-start | bytes 196616 | tf_op jit(solution)/shard_map/ppermute | solution.py:147
  167.0 1.6 collective-permute-start.53
  171.6 1.7 collective-permute-start.46
  174.0 1.9 collective-permute-start.54
  178.3 2.6 %collective-permute-start.49 = (f16[2,64,256]{2,1,0:T(8,128)(2,1)S(1)}, f16[2,64,256]{2,1,0:T(8,128)(2,1)S(1)}, u32[]{:S(2)}, u32[]{:S(2)}) collective-permute-start(f16[2,64,256]{2,1,0:T(8,128)(2,1)S(1)} %reshape.147), channel_id=1, source_target_pairs={{0,6},{1,7},{2,4},{3,5},{4,2},{5,3},{6,0},{7,1},{8,14},{9,15},{10,... | collective-permute-start | bytes 196616 | tf_op jit(solution)/shard_map/ppermute | solution.py:147
  181.2 1.7 collective-permute-start.56
  183.0 2.6 %collective-permute-start.57 = (f16[2,2,64,256]{3,2,1,0:T(8,128)(2,1)S(1)}, f16[2,2,64,256]{3,2,1,0:T(8,128)(2,1)S(1)}, u32[]{:S(2)}, u32[]{:S(2)}) collective-permute-start(f16[2,2,64,256]{3,2,1,0:T(8,128)(2,1)S(1)} %get-tuple-element.50), channel_id=1, source_target_pairs={{0,6},{1,7},{2,4},{3,5},{4,2},{5,3},{6,0},{7,1},{8,14},{9,15},{10,... | collective-permute-start | bytes 393224 | tf_op jit(solution)/shard_map/ppermute | solution.py:147
  188.5 6.7 %collective-permute-done.56 = f16[2,2,64,256]{3,2,1,0:T(8,128)(2,1)S(1)} collective-permute-done((f16[2,2,64,256]{3,2,1,0:T(8,128)(2,1)S(1)}, f16[2,2,64,256]{3,2,1,0:T(8,128)(2,1)S(1)}, u32[]{:S(2)}, u32[]{:S(2)}) %collective-permute-start.56) | collective-permute-done | bytes 131104 | tf_op jit(solution)/shard_map/ppermute | solution.py:147
  196.5 1.7 update.1
  (190 shorter events, 47.7 us)
Async XLA Ops:
  1.8 10.0 %collective-permute-start.22 = (bf16[2,64,256]{2,1,0:T(8,128)(2,1)}, bf16[2,64,256]{2,1,0:T(8,128)(2,1)S(1)}, u32[]{:S(2)}, u32[]{:S(2)}) collective-permute-start(bf16[2,64,256]{2,1,0:T(8,128)(2,1)} %get-tuple-element.17), channel_id=1, source_target_pairs={{0,2},{1,3},{2,0},{3,1},{4,6},{5,7},{6,4},{7,5},{8,10},{9,11},{10,... | collective-permute-start | bytes 196616 | tf_op jit(solution)/shard_map/ppermute | solution.py:147
  7.4 9.2 %collective-permute-start.29 = (bf16[2,64,256]{2,1,0:T(8,128)(2,1)}, bf16[2,64,256]{2,1,0:T(8,128)(2,1)S(1)}, u32[]{:S(2)}, u32[]{:S(2)}) collective-permute-start(bf16[2,64,256]{2,1,0:T(8,128)(2,1)} %get-tuple-element.18), channel_id=1, source_target_pairs={{0,2},{1,3},{2,0},{3,1},{4,6},{5,7},{6,4},{7,5},{8,10},{9,11},{10,... | collective-permute-start | bytes 196616 | tf_op jit(solution)/shard_map/ppermute | solution.py:147
  8.3 10.3 %collective-permute-start.30 = (bf16[2,64,256]{2,1,0:T(8,128)(2,1)}, bf16[2,64,256]{2,1,0:T(8,128)(2,1)S(1)}, u32[]{:S(2)}, u32[]{:S(2)}) collective-permute-start(bf16[2,64,256]{2,1,0:T(8,128)(2,1)} %get-tuple-element.18), channel_id=1, source_target_pairs={{0,4},{1,5},{2,6},{3,7},{4,0},{5,1},{6,2},{7,3},{8,12},{9,13},{10,... | collective-permute-start | bytes 196616 | tf_op jit(solution)/shard_map/ppermute | solution.py:147
  15.1 10.4 %collective-permute-start.25 = (bf16[4,2,64,256]{3,2,1,0:T(8,128)(2,1)S(1)}, bf16[4,2,64,256]{3,2,1,0:T(8,128)(2,1)S(1)}, u32[]{:S(2)}, u32[]{:S(2)}) collective-permute-start(bf16[4,2,64,256]{3,2,1,0:T(8,128)(2,1)S(1)} %get-tuple-element.41), channel_id=1, source_target_pairs={{0,1},{1,0},{2,3},{3,2},{4,5},{5,4},{6,7},{7,6},{8,9},{9,8},{10,11... | collective-permute-start | bytes 786440 | tf_op jit(solution)/shard_map/ppermute | solution.py:147
  30.6 24.5 %collective-permute-start.27 = (bf16[2,4,2,64,256]{4,3,2,1,0:T(8,128)(2,1)S(1)}, bf16[2,4,2,64,256]{4,3,2,1,0:T(8,128)(2,1)S(1)}, u32[]{:S(2)}, u32[]{:S(2)}) collective-permute-start(bf16[2,4,2,64,256]{4,3,2,1,0:T(8,128)(2,1)S(1)} %pad_maximum_fusion.2.refs_0_), channel_id=1, source_target_pairs={{0,16},{1,17},{2,18},{3,19},{4,20},{5,21},{6,22},{7,23},{8,24},{9,... | collective-permute-start | bytes 1572872 | tf_op jit(solution)/shard_map/ppermute | solution.py:147
  33.2 22.9 %collective-permute-start.26 = (bf16[2,4,2,64,256]{4,3,2,1,0:T(8,128)(2,1)S(1)}, bf16[2,4,2,64,256]{4,3,2,1,0:T(8,128)(2,1)S(1)}, u32[]{:S(2)}, u32[]{:S(2)}) collective-permute-start(bf16[2,4,2,64,256]{4,3,2,1,0:T(8,128)(2,1)S(1)} %pad_maximum_fusion.2.refs_0_), channel_id=1, source_target_pairs={{0,8},{1,9},{2,10},{3,11},{4,12},{5,13},{6,14},{7,15},{8,0},{9,1},... | collective-permute-start | bytes 1572872 | tf_op jit(solution)/shard_map/ppermute | solution.py:147
  33.2 22.0 %collective-permute-start.33 = (bf16[2,4,2,64,256]{4,3,2,1,0:T(8,128)(2,1)S(1)}, bf16[2,4,2,64,256]{4,3,2,1,0:T(8,128)(2,1)S(1)}, u32[]{:S(2)}, u32[]{:S(2)}) collective-permute-start(bf16[2,4,2,64,256]{4,3,2,1,0:T(8,128)(2,1)S(1)} %pad_maximum_fusion.3.refs_4_), channel_id=1, source_target_pairs={{0,1},{1,0},{2,3},{3,2},{4,5},{5,4},{6,7},{7,6},{8,9},{9,8},{10,11... | collective-permute-start | bytes 1572872 | tf_op jit(solution)/shard_map/ppermute | solution.py:147
  34.5 13.2 %collective-permute-start.10 = (bf16[4,2,64,256]{3,2,1,0:T(8,128)(2,1)S(1)}, bf16[4,2,64,256]{3,2,1,0:T(8,128)(2,1)S(1)}, u32[]{:S(2)}, u32[]{:S(2)}) collective-permute-start(bf16[4,2,64,256]{3,2,1,0:T(8,128)(2,1)S(1)} %get-tuple-element.46), channel_id=1, source_target_pairs={{0,16},{1,17},{2,18},{3,19},{4,20},{5,21},{6,22},{7,23},{8,24},{9,... | collective-permute-start | bytes 786440 | tf_op jit(solution)/shard_map/ppermute | solution.py:147
  35.3 17.8 %collective-permute-start.3 = (bf16[4,2,64,256]{3,2,1,0:T(8,128)(2,1)S(1)}, bf16[4,2,64,256]{3,2,1,0:T(8,128)(2,1)S(1)}, u32[]{:S(2)}, u32[]{:S(2)}) collective-permute-start(bf16[4,2,64,256]{3,2,1,0:T(8,128)(2,1)S(1)} %get-tuple-element.48), channel_id=1, source_target_pairs={{0,1},{1,0},{2,3},{3,2},{4,5},{5,4},{6,7},{7,6},{8,9},{9,8},{10,11... | collective-permute-start | bytes 786440 | tf_op jit(solution)/shard_map/ppermute | solution.py:147
  47.6 10.6 %collective-permute-start.34 = (bf16[2,4,2,64,256]{4,3,2,1,0:T(8,128)(2,1)S(1)}, bf16[2,4,2,64,256]{4,3,2,1,0:T(8,128)(2,1)S(1)}, u32[]{:S(2)}, u32[]{:S(2)}) collective-permute-start(bf16[2,4,2,64,256]{4,3,2,1,0:T(8,128)(2,1)S(1)} %pad_maximum_fusion.3.refs_4_), channel_id=1, source_target_pairs={{0,8},{1,9},{2,10},{3,11},{4,12},{5,13},{6,14},{7,15},{8,0},{9,1},... | collective-permute-start | bytes 1572872 | tf_op jit(solution)/shard_map/ppermute | solution.py:147
  53.2 13.9 %collective-permute-start.11 = (bf16[2,4,2,64,256]{4,3,2,1,0:T(8,128)(2,1)}, bf16[2,4,2,64,256]{4,3,2,1,0:T(8,128)(2,1)}, u32[]{:S(2)}, u32[]{:S(2)}) collective-permute-start(bf16[2,4,2,64,256]{4,3,2,1,0:T(8,128)(2,1)} %pad_maximum_fusion.1.refs_4_), channel_id=1, source_target_pairs={{0,1},{1,0},{2,3},{3,2},{4,5},{5,4},{6,7},{7,6},{8,9},{9,8},{10,11... | collective-permute-start | bytes 1572872 | tf_op jit(solution)/shard_map/ppermute | solution.py:147
  55.2 13.6 %collective-permute-start.5 = (bf16[2,4,2,64,256]{4,3,2,1,0:T(8,128)(2,1)}, bf16[2,4,2,64,256]{4,3,2,1,0:T(8,128)(2,1)}, u32[]{:S(2)}, u32[]{:S(2)}) collective-permute-start(bf16[2,4,2,64,256]{4,3,2,1,0:T(8,128)(2,1)} %pad_maximum_fusion.refs_0_), channel_id=1, source_target_pairs={{0,16},{1,17},{2,18},{3,19},{4,20},{5,21},{6,22},{7,23},{8,24},{9,... | collective-permute-start | bytes 1572872 | tf_op jit(solution)/shard_map/ppermute | solution.py:147
  55.2 13.6 %collective-permute-start.28 = (bf16[2,4,2,64,256]{4,3,2,1,0:T(8,128)(2,1)S(1)}, bf16[2,4,2,64,256]{4,3,2,1,0:T(8,128)(2,1)}, u32[]{:S(2)}, u32[]{:S(2)}) collective-permute-start(bf16[2,4,2,64,256]{4,3,2,1,0:T(8,128)(2,1)S(1)} %collective-permute-done.27.refs_2_), channel_id=1, source_target_pairs={{0,8},{1,9},{2,10},{3,11},{4,12},{5,13},{6,14},{7,15},{8,0},{9,1},... | collective-permute-start | bytes 1572872 | tf_op jit(solution)/shard_map/ppermute | solution.py:147
  56.9 12.4 %collective-permute-start.35 = (bf16[2,4,2,64,256]{4,3,2,1,0:T(8,128)(2,1)S(1)}, bf16[2,4,2,64,256]{4,3,2,1,0:T(8,128)(2,1)S(1)}, u32[]{:S(2)}, u32[]{:S(2)}) collective-permute-start(bf16[2,4,2,64,256]{4,3,2,1,0:T(8,128)(2,1)S(1)} %collective-permute-done.33.refs_5_), channel_id=1, source_target_pairs={{0,8},{1,9},{2,10},{3,11},{4,12},{5,13},{6,14},{7,15},{8,0},{9,1},... | collective-permute-start | bytes 1572872 | tf_op jit(solution)/shard_map/ppermute | solution.py:147
  59.1 38.8 %collective-permute-start.12 = (bf16[2,4,2,64,256]{4,3,2,1,0:T(8,128)(2,1)}, bf16[2,4,2,64,256]{4,3,2,1,0:T(8,128)(2,1)S(1)}, u32[]{:S(2)}, u32[]{:S(2)}) collective-permute-start(bf16[2,4,2,64,256]{4,3,2,1,0:T(8,128)(2,1)} %pad_maximum_fusion.1.refs_4_), channel_id=1, source_target_pairs={{0,8},{1,9},{2,10},{3,11},{4,12},{5,13},{6,14},{7,15},{8,0},{9,1},... | collective-permute-start | bytes 1572872 | tf_op jit(solution)/shard_map/ppermute | solution.py:147
  67.0 30.8 %collective-permute-start.4 = (bf16[2,4,2,64,256]{4,3,2,1,0:T(8,128)(2,1)}, bf16[2,4,2,64,256]{4,3,2,1,0:T(8,128)(2,1)S(1)}, u32[]{:S(2)}, u32[]{:S(2)}) collective-permute-start(bf16[2,4,2,64,256]{4,3,2,1,0:T(8,128)(2,1)} %pad_maximum_fusion.refs_0_), channel_id=1, source_target_pairs={{0,8},{1,9},{2,10},{3,11},{4,12},{5,13},{6,14},{7,15},{8,0},{9,1},... | collective-permute-start | bytes 1572872 | tf_op jit(solution)/shard_map/ppermute | solution.py:147
  68.8 29.1 %collective-permute-start.13 = (bf16[2,4,2,64,256]{4,3,2,1,0:T(8,128)(2,1)}, bf16[2,4,2,64,256]{4,3,2,1,0:T(8,128)(2,1)S(1)}, u32[]{:S(2)}, u32[]{:S(2)}) collective-permute-start(bf16[2,4,2,64,256]{4,3,2,1,0:T(8,128)(2,1)} %collective-permute-done.11.refs_5_), channel_id=1, source_target_pairs={{0,8},{1,9},{2,10},{3,11},{4,12},{5,13},{6,14},{7,15},{8,0},{9,1},... | collective-permute-start | bytes 1572872 | tf_op jit(solution)/shard_map/ppermute | solution.py:147
  68.8 29.1 %collective-permute-start.6 = (bf16[2,4,2,64,256]{4,3,2,1,0:T(8,128)(2,1)}, bf16[2,4,2,64,256]{4,3,2,1,0:T(8,128)(2,1)S(1)}, u32[]{:S(2)}, u32[]{:S(2)}) collective-permute-start(bf16[2,4,2,64,256]{4,3,2,1,0:T(8,128)(2,1)} %collective-permute-done.5.refs_2_), channel_id=1, source_target_pairs={{0,8},{1,9},{2,10},{3,11},{4,12},{5,13},{6,14},{7,15},{8,0},{9,1},... | collective-permute-start | bytes 1572872 | tf_op jit(solution)/shard_map/ppermute | solution.py:147
  97.8 23.0 %collective-permute-start.36 = (f32[16,2,64,256]{3,2,1,0:T(8,128)}, f32[16,2,64,256]{3,2,1,0:T(8,128)}, u32[]{:S(2)}, u32[]{:S(2)}) collective-permute-start(f32[16,2,64,256]{3,2,1,0:T(8,128)} %get-tuple-element.20), channel_id=1, source_target_pairs={{0,8},{1,9},{2,10},{3,11},{4,12},{5,13},{6,14},{7,15},{8,0},{9,1},... | collective-permute-start | bytes 6291464 | tf_op jit(solution)/shard_map/ppermute | solution.py:147
  128.3 14.6 %collective-permute-start.37 = (f16[8,2,1,32,256]{4,3,1,0,2:T(8,128)(2,1)S(1)}, f16[8,2,1,32,256]{4,3,1,0,2:T(8,128)(2,1)S(1)}, u32[]{:S(2)}, u32[]{:S(2)}) collective-permute-start(f16[8,2,1,32,256]{4,3,1,0,2:T(8,128)(2,1)S(1)} %dynamic-slice_bitcast_fusion), channel_id=1, source_target_pairs={{0,16},{1,17},{2,18},{3,19},{4,20},{5,21},{6,22},{7,23},{8,24},{9,... | collective-permute-start | bytes 786440 | tf_op jit(solution)/shard_map/ppermute | solution.py:147
  135.8 9.4 %collective-permute-start.17 = (f16[4,2,2,32,256]{4,3,1,2,0:T(8,128)(2,1)S(1)}, f16[4,2,2,32,256]{4,3,1,2,0:T(8,128)(2,1)S(1)}, u32[]{:S(2)}, u32[]{:S(2)}) collective-permute-start(f16[4,2,2,32,256]{4,3,1,2,0:T(8,128)(2,1)S(1)} %bitcast.166), channel_id=1, source_target_pairs={{0,1},{1,0},{2,3},{3,2},{4,5},{5,4},{6,7},{7,6},{8,9},{9,8},{10,11... | collective-permute-start | bytes 786440 | tf_op jit(solution)/shard_map/ppermute | solution.py:147
  136.0 12.5 %collective-permute-start.15 = (f16[8,2,1,32,256]{4,3,1,0,2:T(8,128)(2,1)S(1)}, f16[8,2,1,32,256]{4,3,1,0,2:T(8,128)(2,1)S(1)}, u32[]{:S(2)}, u32[]{:S(2)}) collective-permute-start(f16[8,2,1,32,256]{4,3,1,0,2:T(8,128)(2,1)S(1)} %dynamic-slice_bitcast_fusion.1), channel_id=1, source_target_pairs={{0,16},{1,17},{2,18},{3,19},{4,20},{5,21},{6,22},{7,23},{8,24},{9,... | collective-permute-start | bytes 786440 | tf_op jit(solution)/shard_map/ppermute | solution.py:147
  136.6 14.6 %collective-permute-start.40 = (f16[4,2,1,32,256]{4,3,1,2,0:T(8,128)(2,1)S(1)}, f16[4,2,1,32,256]{4,3,1,2,0:T(8,128)(2,1)S(1)}, u32[]{:S(2)}, u32[]{:S(2)}) collective-permute-start(f16[4,2,1,32,256]{4,3,1,2,0:T(8,128)(2,1)S(1)} %constant_dynamic-slice_fusion.10), channel_id=1, source_target_pairs={{0,16},{1,17},{2,18},{3,19},{4,20},{5,21},{6,22},{7,23},{8,24},{9,... | collective-permute-start | bytes 393224 | tf_op jit(solution)/shard_map/ppermute | solution.py:147
  145.3 15.0 %collective-permute-start.18 = (f16[4,2,1,32,256]{4,3,1,2,0:T(8,128)(2,1)S(1)}, f16[4,2,1,32,256]{4,3,1,2,0:T(8,128)(2,1)S(1)}, u32[]{:S(2)}, u32[]{:S(2)}) collective-permute-start(f16[4,2,1,32,256]{4,3,1,2,0:T(8,128)(2,1)S(1)} %constant_dynamic-slice_fusion.13), channel_id=1, source_target_pairs={{0,16},{1,17},{2,18},{3,19},{4,20},{5,21},{6,22},{7,23},{8,24},{9,... | collective-permute-start | bytes 393224 | tf_op jit(solution)/shard_map/ppermute | solution.py:147
  148.7 11.7 %collective-permute-start.16 = (f16[4,2,1,32,256]{4,3,1,2,0:T(8,128)(2,1)S(1)}, f16[4,2,1,32,256]{4,3,1,2,0:T(8,128)(2,1)S(1)}, u32[]{:S(2)}, u32[]{:S(2)}) collective-permute-start(f16[4,2,1,32,256]{4,3,1,2,0:T(8,128)(2,1)S(1)} %dynamic-slice_bitcast_fusion.3), channel_id=1, source_target_pairs={{0,1},{1,0},{2,3},{3,2},{4,5},{5,4},{6,7},{7,6},{8,9},{9,8},{10,11... | collective-permute-start | bytes 393224 | tf_op jit(solution)/shard_map/ppermute | solution.py:147
  151.5 13.5 %collective-permute-start.41 = (f16[2,64,256]{2,1,0:T(8,128)(2,1)S(1)}, f16[2,64,256]{2,1,0:T(8,128)(2,1)S(1)}, u32[]{:S(2)}, u32[]{:S(2)}) collective-permute-start(f16[2,64,256]{2,1,0:T(8,128)(2,1)S(1)} %get-tuple-element.35), channel_id=1, source_target_pairs={{0,2},{1,3},{2,0},{3,1},{4,6},{5,7},{6,4},{7,5},{8,10},{9,11},{10,... | collective-permute-start | bytes 196616 | tf_op jit(solution)/shard_map/ppermute | solution.py:147
  151.5 13.4 %collective-permute-start.42 = (f16[2,64,256]{2,1,0:T(8,128)(2,1)S(1)}, f16[2,64,256]{2,1,0:T(8,128)(2,1)S(1)}, u32[]{:S(2)}, u32[]{:S(2)}) collective-permute-start(f16[2,64,256]{2,1,0:T(8,128)(2,1)S(1)} %get-tuple-element.36), channel_id=1, source_target_pairs={{0,4},{1,5},{2,6},{3,7},{4,0},{5,1},{6,2},{7,3},{8,12},{9,13},{10,... | collective-permute-start | bytes 196616 | tf_op jit(solution)/shard_map/ppermute | solution.py:147
  161.1 8.6 %collective-permute-start.20 = (f16[2,64,256]{2,1,0:T(8,128)(2,1)S(1)}, f16[2,64,256]{2,1,0:T(8,128)(2,1)S(1)}, u32[]{:S(2)}, u32[]{:S(2)}) collective-permute-start(f16[2,64,256]{2,1,0:T(8,128)(2,1)S(1)} %get-tuple-element.43), channel_id=1, source_target_pairs={{0,4},{1,5},{2,6},{3,7},{4,0},{5,1},{6,2},{7,3},{8,12},{9,13},{10,... | collective-permute-start | bytes 196616 | tf_op jit(solution)/shard_map/ppermute | solution.py:147
  176.9 8.7 %collective-permute-start.48 = (f16[2,64,256]{2,1,0:T(8,128)(2,1)S(1)}, f16[2,64,256]{2,1,0:T(8,128)(2,1)S(1)}, u32[]{:S(2)}, u32[]{:S(2)}) collective-permute-start(f16[2,64,256]{2,1,0:T(8,128)(2,1)S(1)} %reshape.147), channel_id=1, source_target_pairs={{0,4},{1,5},{2,6},{3,7},{4,0},{5,1},{6,2},{7,3},{8,12},{9,13},{10,... | collective-permute-start | bytes 196616 | tf_op jit(solution)/shard_map/ppermute | solution.py:147
  181.2 14.0 %collective-permute-start.56 = (f16[2,2,64,256]{3,2,1,0:T(8,128)(2,1)S(1)}, f16[2,2,64,256]{3,2,1,0:T(8,128)(2,1)S(1)}, u32[]{:S(2)}, u32[]{:S(2)}) collective-permute-start(f16[2,2,64,256]{3,2,1,0:T(8,128)(2,1)S(1)} %get-tuple-element.50), channel_id=1, source_target_pairs={{0,4},{1,5},{2,6},{3,7},{4,0},{5,1},{6,2},{7,3},{8,12},{9,13},{10,... | collective-permute-start | bytes 393224 | tf_op jit(solution)/shard_map/ppermute | solution.py:147
  183.0 12.3 %collective-permute-start.57 = (f16[2,2,64,256]{3,2,1,0:T(8,128)(2,1)S(1)}, f16[2,2,64,256]{3,2,1,0:T(8,128)(2,1)S(1)}, u32[]{:S(2)}, u32[]{:S(2)}) collective-permute-start(f16[2,2,64,256]{3,2,1,0:T(8,128)(2,1)S(1)} %get-tuple-element.50), channel_id=1, source_target_pairs={{0,6},{1,7},{2,4},{3,5},{4,2},{5,3},{6,0},{7,1},{8,14},{9,15},{10,... | collective-permute-start | bytes 393224 | tf_op jit(solution)/shard_map/ppermute | solution.py:147
  185.7 9.8 %collective-permute-start.50 = (f16[4,2,64,256]{3,2,1,0:T(8,128)(2,1)S(1)}, f16[4,2,64,256]{3,2,1,0:T(8,128)(2,1)S(1)}, u32[]{:S(2)}, u32[]{:S(2)}) collective-permute-start(f16[4,2,64,256]{3,2,1,0:T(8,128)(2,1)S(1)} %get-tuple-element.34), channel_id=1, source_target_pairs={{0,1},{1,0},{2,3},{3,2},{4,5},{5,4},{6,7},{7,6},{8,9},{9,8},{10,11... | collective-permute-start | bytes 786440 | tf_op jit(solution)/shard_map/ppermute | solution.py:147
  (47 other events, 373.0 us)

commit v4 on v3

--- a/solution.py
+++ b/solution.py
@@ -159,31 +159,31 @@
     return (own.astype(jnp.float32) + other.astype(jnp.float32)).astype(value.dtype)
 
 
-def reduce_blocks(keep, send, nodes, cores, scale):
-    total = nodes * cores
-    node_index = lax.axis_index("node")
-    core_index = lax.axis_index("cores")
+def add_other_core(keep, send, nodes, cores, scale):
+    got = swap(send, cores, nodes * cores)
     slots, inner, rows, tile = keep.shape
-    got = swap(send, cores, total)
     part = ((keep + got) * scale).astype(jnp.float16).reshape(cores, slots // cores, inner, rows, tile)
-
-    def over_inner(value):
-        mask, index = 2 * cores, node_index // 2
-        while value.shape[2] > 1:
-            value = halve(value, index % 2, 2, mask, total)
-            mask, index = mask * 2, index // 2
-        return value
-
-    def over_low(value):
-        return halve(value, core_index % 2, 0, 1, total)
-
-    upper = over_low(over_inner(part[:, :, :, :rows // 2]))
-    lower = over_inner(over_low(part[:, :, :, rows // 2:]))
+    return part[:, :, :, :rows // 2], part[:, :, :, rows // 2:]
+
+
+def over_inner(value, nodes, cores):
+    mask, index = 2 * cores, lax.axis_index("node") // 2
+    while value.shape[2] > 1:
+        value = halve(value, index % 2, 2, mask, nodes * cores)
+        mask, index = mask * 2, index // 2
+    return value
+
+
+def over_low(value, nodes, cores):
+    return halve(value, lax.axis_index("cores") % 2, 0, 1, nodes * cores)
+
+
+def over_far(upper, lower, nodes, cores, scale):
     part = jnp.concatenate([upper, lower], axis=3)[:, :, 0]
-    at = core_index // 2
+    at = lax.axis_index("cores") // 2
     mine = pick(part, at, 0).astype(jnp.float32)
     for step in range(1, part.shape[0]):
-        mine = mine + swap(pick(part, at ^ step, 0), 2 * step, total).astype(jnp.float32)
+        mine = mine + swap(pick(part, at ^ step, 0), 2 * step, nodes * cores).astype(jnp.float32)
     return mine * (0.5 / scale)
 
 
@@ -198,9 +198,9 @@
 
 
 def lower_kernel(partner_ref, amps_ref, *out_refs):
-    for g, both in enumerate(pair_groups(partner_ref, amps_ref.shape[1])):
+    for out_ref, both in zip(out_refs, pair_groups(partner_ref, amps_ref.shape[1])):
         for role, p in enumerate(both):
-            out_refs[2 * g + role][...] = amps_ref[:, p].astype(jnp.bfloat16)
+            out_ref[role] = amps_ref[:, p].astype(jnp.bfloat16)
 
 
 def lower(partner, amplitudes):
@@ -208,41 +208,45 @@
     vmem = pl.BlockSpec(memory_space=pltpu.VMEM)
     return pl.pallas_call(
         lower_kernel,
-        out_shape=(jax.ShapeDtypeStruct((slots_here, rows, tile), jnp.bfloat16),) * pairs,
+        out_shape=(jax.ShapeDtypeStruct((2, slots_here, rows, tile), jnp.bfloat16),) * (pairs // 2),
         in_specs=[pl.BlockSpec(memory_space=pltpu.SMEM), vmem],
-        out_specs=(vmem,) * pairs,
+        out_specs=(vmem,) * (pairs // 2),
         name="lower",
     )(partner, amplitudes)
 
 
 def spread_far(part, cores, total):
-    return jnp.stack([part] + [swap(part, 2 * step, total) for step in range(1, cores // 2)])
-
-
-def spread_first(part, nodes, cores):
-    total = nodes * cores
-    part = spread_far(part, cores, total)
-    pieces = {0: jnp.stack([part, swap(part, 1, total)])}
-    bit = nodes // 2
-    while bit:
-        pieces.update({other | bit: swap(piece, bit * cores, total) for other, piece in pieces.items()})
-        bit //= 2
-    return [pieces[other] for other in range(nodes)]
-
-
-def spread_second(part, nodes, cores):
-    total = nodes * cores
-    pieces = {0: spread_far(part, cores, total)}
+    return [part] + [swap(part, 2 * step, total) for step in range(1, cores // 2)]
+
+
+def spread_inner(parts, nodes, cores):
+    total = nodes * cores
+    first = jnp.stack([part[0] for part in parts])
+    first = jnp.stack([first, swap(first, 1, total)])
+    pieces = {0: jnp.stack([part[1] for part in parts])}
     bit = nodes // 2
     while bit > 1:
         pieces.update({other | bit: swap(piece, bit * cores, total) for other, piece in pieces.items()})
         bit //= 2
-    near = jnp.stack([pieces[2 * upper] for upper in range(nodes // 2)])
-    far = swap(near, 1, total)
-    return [near, far, swap(near, cores, total), swap(far, cores, total)]
-
-
-def turn_blocks(mine, far_first, nodes, cores, scale):
+    return first, jnp.stack([pieces[2 * upper] for upper in range(nodes // 2)])
+
+
+def spread_outer(first, second, nodes, cores):
+    total = nodes * cores
+    pieces = {0: first}
+    bit = nodes // 2
+    while bit > 1:
+        pieces.update({other | bit: swap(piece, bit * cores, total) for other, piece in pieces.items()})
+        bit //= 2
+    return [pieces[2 * upper] for upper in range(1, nodes // 2)], swap(second, 1, total)
+
+
+def spread_last(first, second, nodes, cores):
+    total = nodes * cores
+    return [swap(piece, cores, total) for piece in first], [swap(piece, cores, total) for piece in second]
+
+
+def turn_blocks(mine, nodes, cores, scale):
     total = nodes * cores
     slots_here, rows, tile = mine.shape
     node_index = lax.axis_index("node")
@@ -252,13 +256,12 @@
     pieces += [swap(pick(turned, node_index ^ step, 0), step * cores, total) for step in range(1, nodes)]
     pieces = jnp.stack(pieces)
     block = jnp.stack([pick(pieces, node_index ^ n, 0) for n in range(nodes)])
-    block = block.reshape(nodes, rows, slots_here, rows).transpose(2, 1, 0, 3).reshape(slots_here, rows, tile)
-    if far_first:
-        near = spread_far(block, cores, total)
-        every = jnp.stack([near, swap(near, 1, total)], axis=1)
-    else:
-        every = spread_far(jnp.stack([block, swap(block, 1, total)]), cores, total)
-    return every.reshape(cores, slots_here, rows, tile).astype(jnp.float32) * (1.0 / scale)
+    return block.reshape(nodes, rows, slots_here, rows).transpose(2, 1, 0, 3).reshape(slots_here, rows, tile)
+
+
+def every_block(near, nodes, cores, scale):
+    every = jnp.stack([near, swap(near, 1, nodes * cores)], axis=1)
+    return every.reshape((cores,) + near.shape[1:]).astype(jnp.float32) * (1.0 / scale)
 
 
 def update_kernel(side, owner_ref, partner_ref, pair_ref, energy_ref, column_ref, amps_ref, *refs):
@@ -306,16 +309,51 @@
 
 def body(nodes, cores, fitted, fit_mask, tasks, owner_map, partner, amplitudes, pair_energy, virt_energy):
     scale = 2.0 ** -9
+    total = nodes * cores
     parts = lower(partner, amplitudes)
-    groups = len(parts) // 2
-    first = [spread_first(parts[2 * g], nodes, cores) for g in range(groups)]
-    second = [spread_second(parts[2 * g + 1], nodes, cores) for g in range(groups)]
-    straight, crossed = [], []
+    groups = len(parts)
+    barrier = lax.optimization_barrier
+
+    far, inner, outer = [], [], []
     for g in range(groups):
-        keep, send = ladder_terms(fit_mask, tasks, owner_map, fitted, first[g], second[g], nodes, cores)
-        mine = reduce_blocks(keep, send, nodes, cores, scale)
-        straight.append(mine)
-        crossed.append(turn_blocks(mine, g == 0, nodes, cores, scale))
+        part = parts[g]
+        if g:
+            part, far[g - 1] = barrier((part, far[g - 1]))
+        far.append(spread_far(part, cores, total))
+    for g in range(groups):
+        inner.append(spread_inner(far[g], nodes, cores))
+        outer.append(spread_outer(*inner[g], nodes, cores))
+    sums = []
+    for g in range(groups):
+        first = [inner[g][0]] + outer[g][0]
+        second = [inner[g][1], outer[g][1]]
+        if g:
+            (first, second), sums[g - 1] = barrier(((first, second), sums[g - 1]))
+        first_far, second_far = spread_last(first, second, nodes, cores)
+        first = [piece for pair in zip(first, first_far) for piece in pair]
+        sums.append(ladder_terms(fit_mask, tasks, owner_map, fitted, first, second + second_far, nodes, cores))
+    stages = [
+        lambda v: add_other_core(*v, nodes, cores, scale),
+        lambda v: (over_inner(v[0], nodes, cores), over_low(v[1], nodes, cores)),
+        lambda v: (over_low(v[0], nodes, cores), over_inner(v[1], nodes, cores)),
+        lambda v: over_far(*v, nodes, cores, scale),
+        lambda v: turn_blocks(v, nodes, cores, scale),
+        lambda v: jnp.stack(spread_far(v, cores, total)),
+        lambda v: every_block(v, nodes, cores, scale),
+    ]
+    state, straight = list(sums), [None] * groups
+    for step in range(len(stages) + groups - 1):
+        live = [g for g in range(groups) if 0 <= step - g < len(stages)]
+        for g in live:
+            state[g] = stages[step - g](state[g])
+            if step - g == 3:
+                straight[g] = state[g]
+        upcoming = [g for g in range(groups) if 0 <= step + 1 - g < len(stages)]
+        if len(upcoming) > 1 and step:
+            tied = barrier(tuple(state[g] for g in upcoming))
+            for g, value in zip(upcoming, tied):
+                state[g] = value
+    crossed = state
     return update(owner_map, partner, pair_energy, virt_energy, amplitudes, straight, crossed)
 
 

time: 199 us -> 208 us (1.045)
  waiting for transfers between devices: 46.1 us -> 74.4 us
  starting transfers between devices: 80.2 us -> 56.4 us
  Pallas kernels: 47.4 us -> 58.4 us
  local copies, waits for them, and re-layouts: 14.6 us -> 7.69 us
    ppermute x58 -> x52, waiting for transfers between devices: 46.1 us -> 74.4 us  [swap(): return lax.ppermute(array, AXES, [(i, i ^ mask) for i in range(total)])]
    ppermute x58 -> x52, starting transfers between devices: 80.2 us -> 56.4 us  [swap(): return lax.ppermute(array, AXES, [(i, i ^ mask) for i in range(total)])]
    pallas_call x2, Pallas kernels: 43.9 us -> 54.9 us  [ladder_terms(): pl.pallas_call(functools.partial(ladder_kernel, dims), out_shape=(part, p...]
    unnamed x45 -> x21, local copies, waits for them, and re-layouts: 11.6 us -> 2.28 us
  transfers between devices with their start and end apart: 58 -> 52, of which waited for: 17 -> 27; matrix products, arithmetic and copies ran while one was open for 5% -> 6% of each run, Pallas kernels for 22% -> 26%
where the time goes in v4:
time: 208 us
  waiting for transfers between devices  74.4 us (36%)
  Pallas kernels  58.4 us (28%)
  starting transfers between devices  56.4 us (27%)
  other arithmetic  10.3 us (5%)
  local copies, waits for them, and re-layouts  7.69 us (4%)
    ppermute x52, waiting for transfers between devices, swap(): return lax.ppermute(array, AXES, [(i, i ^ mask) for i in range(total)])  74.4 us
    ppermute x52, starting transfers between devices, swap(): return lax.ppermute(array, AXES, [(i, i ^ mask) for i in range(total)])  56.4 us
    pallas_call x2, Pallas kernels, ladder_terms(): pl.pallas_call(functools.partial(ladder_kernel, dims), out_shape=(part, p...  54.9 us
    convert_element_type x2, other arithmetic, add_other_core(): ((keep + got) * scale).astype(jnp.float16)  4.83 us
  transfers between devices with their start and end apart: 52, of which 27 were waited for; matrix products, arithmetic and copies ran while one was open for 6% of the time, Pallas kernels for 26%

profile of v4, /device:TPU:0, one launch (start us, length us, event | category | flops | bytes accessed | tf_op | source)
XLA Modules:
  0.0 207.9 jit_solution(18038959814122868548)
XLA Ops:
  0.0 1.8 lower.1
  1.8 3.0 %collective-permute-start = (bf16[2,2,64,256]{3,2,1,0:T(8,128)(2,1)}, bf16[2,2,64,256]{3,2,1,0:T(8,128)(2,1)S(1)}, u32[]{:S(2)}, u32[]{:S(2)}) collective-permute-start(bf16[2,2,64,256]{3,2,1,0:T(8,128)(2,1)} %get-tuple-element.40), channel_id=1, source_target_pairs={{0,2},{1,3},{2,0},{3,1},{4,6},{5,7},{6,4},{7,5},{8,10},{9,11},{10,... | collective-permute-start | bytes 393224 | tf_op jit(solution)/shard_map/ppermute | solution.py:147
  4.8 2.6 %collective-permute-start.1 = (bf16[2,2,64,256]{3,2,1,0:T(8,128)(2,1)}, bf16[2,2,64,256]{3,2,1,0:T(8,128)(2,1)S(1)}, u32[]{:S(2)}, u32[]{:S(2)}) collective-permute-start(bf16[2,2,64,256]{3,2,1,0:T(8,128)(2,1)} %get-tuple-element.40), channel_id=1, source_target_pairs={{0,4},{1,5},{2,6},{3,7},{4,0},{5,1},{6,2},{7,3},{8,12},{9,13},{10,... | collective-permute-start | bytes 393224 | tf_op jit(solution)/shard_map/ppermute | solution.py:147
  7.4 2.6 %collective-permute-done = bf16[2,2,64,256]{3,2,1,0:T(8,128)(2,1)S(1)} collective-permute-done((bf16[2,2,64,256]{3,2,1,0:T(8,128)(2,1)}, bf16[2,2,64,256]{3,2,1,0:T(8,128)(2,1)S(1)}, u32[]{:S(2)}, u32[]{:S(2)}) %collective-permute-start) | collective-permute-done | bytes 131104 | tf_op jit(solution)/shard_map/ppermute | solution.py:147
  10.0 7.9 %collective-permute-done.1 = bf16[2,2,64,256]{3,2,1,0:T(8,128)(2,1)S(1)} collective-permute-done((bf16[2,2,64,256]{3,2,1,0:T(8,128)(2,1)}, bf16[2,2,64,256]{3,2,1,0:T(8,128)(2,1)S(1)}, u32[]{:S(2)}, u32[]{:S(2)}) %collective-permute-start.1) | collective-permute-done | bytes 131104 | tf_op jit(solution)/shard_map/ppermute | solution.py:147
  18.0 2.3 %collective-permute-start.5 = (bf16[2,2,64,256]{3,2,1,0:T(8,128)(2,1)}, bf16[2,2,64,256]{3,2,1,0:T(8,128)(2,1)S(1)}, u32[]{:S(2)}, u32[]{:S(2)}) collective-permute-start(bf16[2,2,64,256]{3,2,1,0:T(8,128)(2,1)} %get-tuple-element.39), channel_id=1, source_target_pairs={{0,6},{1,7},{2,4},{3,5},{4,2},{5,3},{6,0},{7,1},{8,14},{9,15},{10,... | collective-permute-start | bytes 393224 | tf_op jit(solution)/shard_map/ppermute | solution.py:147
  27.4 3.2 %collective-permute-done.10 = bf16[4,2,64,256]{3,2,1,0:T(8,128)(2,1)S(1)} collective-permute-done((bf16[4,2,64,256]{3,2,1,0:T(8,128)(2,1)S(1)}, bf16[4,2,64,256]{3,2,1,0:T(8,128)(2,1)S(1)}, u32[]{:S(2)}, u32[]{:S(2)}) %collective-permute-start.10) | collective-permute-done | bytes 262176 | tf_op jit(solution)/shard_map/ppermute | solution.py:147
  32.3 2.3 %collective-permute-done.14 = bf16[4,2,64,256]{3,2,1,0:T(8,128)(2,1)S(1)} collective-permute-done((bf16[4,2,64,256]{3,2,1,0:T(8,128)(2,1)S(1)}, bf16[4,2,64,256]{3,2,1,0:T(8,128)(2,1)S(1)}, u32[]{:S(2)}, u32[]{:S(2)}) %collective-permute-start.14) | collective-permute-done | bytes 262176 | tf_op jit(solution)/shard_map/ppermute | solution.py:147
  34.9 2.1 collective-permute-start.6
  37.5 6.0 %collective-permute-done.12.refs_2_ = bf16[2,4,2,64,256]{4,3,2,1,0:T(8,128)(2,1)S(1)} collective-permute-done((bf16[2,4,2,64,256]{4,3,2,1,0:T(8,128)(2,1)S(1)}, bf16[2,4,2,64,256]{4,3,2,1,0:T(8,128)(2,1)S(1)}, u32[]{:S(2)}, u32[]{:S(2)}) %collective-permute-start.12) | collective-permute-done | bytes 524320 | tf_op jit(solution)/shard_map/ppermute | solution.py:147
  43.5 1.9 collective-permute-done.15.refs_5_
  46.3 1.9 collective-permute-done.6
  51.5 4.5 %collective-permute-done.8 = bf16[4,2,64,256]{3,2,1,0:T(8,128)(2,1)} collective-permute-done((bf16[4,2,64,256]{3,2,1,0:T(8,128)(2,1)}, bf16[4,2,64,256]{3,2,1,0:T(8,128)(2,1)}, u32[]{:S(2)}, u32[]{:S(2)}) %collective-permute-start.8) | collective-permute-done | bytes 262176 | tf_op jit(solution)/shard_map/ppermute | solution.py:147
  59.5 26.9 %ladder.2 = (f32[16,2,64,256]{3,2,1,0:T(8,128)S(1)}, f32[16,2,64,256]{3,2,1,0:T(8,128)}) custom-call(s32[16,32]{1,0:T(8,128)S(1)} %copy-done.5, s32[16,2]{1,0:T(8,128)S(1)} %copy.26.tasks_ref, s32[16]{0:T(128)S(1)} %copy-done.3, bf16[16,8,256,256]{3,2,1,0:T(8,128)(2,1)} %fitted_ref.3, bf16[2,4,2,64,256]{4,3,2,1,0:T(8,128)(2,1)S(1)} %pad_maximum_fusion.2.refs_0_, ...), custom_call_target="tpu_custom_call" | custom-call | flops 20000000000 | bytes 31457280 | tf_op jit(solution)/shard_map/ladder/pallas_call | solution.py:124
  93.5 28.0 %ladder.3 = (f32[16,2,64,256]{3,2,1,0:T(8,128)S(1)}, f32[16,2,64,256]{3,2,1,0:T(8,128)}) custom-call(s32[16,32]{1,0:T(8,128)S(1)} %copy-done.5, s32[16,2]{1,0:T(8,128)S(1)} %copy.26.tasks_ref, s32[16]{0:T(128)S(1)} %copy-done.3, bf16[16,8,256,256]{3,2,1,0:T(8,128)(2,1)} %fitted_ref.3, bf16[2,4,2,64,256]{4,3,2,1,0:T(8,128)(2,1)S(1)} %pad_maximum_fusion.refs_0_, ...), custom_call_target="tpu_custom_call" | custom-call | flops 20000000000 | bytes 31457280 | tf_op jit(solution)/shard_map/ladder/pallas_call | solution.py:124
  121.6 2.7 %multiply_convert_fusion.1 = f16[16,2,64,256]{3,2,1,0:T(8,128)(2,1)S(1)} fusion(f32[16,2,64,256]{3,2,1,0:T(8,128)} %copy-done.1, f32[16,2,64,256]{3,2,1,0:T(8,128)} %collective-permute-done.18), kind=kLoop, calls=%fused_computation.1 | loop fusion | flops 1572864 | bytes 5242880 | tf_op jit(solution)/shard_map/convert_element_type | solution.py:165
  125.7 8.6 %collective-permute-done.19 = f16[8,2,1,32,256]{4,3,2,1,0:T(8,128)(2,1)} collective-permute-done((f16[8,2,1,32,256]{4,3,2,1,0:T(8,128)(2,1)}, f16[8,2,1,32,256]{4,3,2,1,0:T(8,128)(2,1)}, u32[]{:S(2)}, u32[]{:S(2)}) %collective-permute-start.19) | collective-permute-done | bytes 262176 | tf_op jit(solution)/shard_map/ppermute | solution.py:147
  135.6 2.1 %multiply_convert_fusion = f16[16,2,64,256]{3,2,1,0:T(8,128)(2,1)S(1)} fusion(f32[16,2,64,256]{3,2,1,0:T(8,128)S(1)} %get-tuple-element.52, f32[16,2,64,256]{3,2,1,0:T(8,128)} %collective-permute-done.25), kind=kLoop, calls=%fused_computation | loop fusion | flops 1572864 | bytes 5242880 | tf_op jit(solution)/shard_map/convert_element_type | solution.py:165
  140.6 2.1 collective-permute-start.29
  144.7 4.2 %collective-permute-done.28 = f16[8,2,1,32,256]{4,3,2,1,0:T(8,128)(2,1)S(1)} collective-permute-done((f16[8,2,1,32,256]{4,3,2,1,0:T(8,128)(2,1)S(1)}, f16[8,2,1,32,256]{4,3,2,1,0:T(8,128)(2,1)S(1)}, u32[]{:S(2)}, u32[]{:S(2)}) %collective-permute-start.28) | collective-permute-done | bytes 262176 | tf_op jit(solution)/shard_map/ppermute | solution.py:147
  149.3 8.9 %collective-permute-start.32 = (f16[2,64,256]{2,1,0:T(8,128)(2,1)S(1)}, f16[2,64,256]{2,1,0:T(8,128)(2,1)S(1)}, u32[]{:S(2)}, u32[]{:S(2)}) collective-permute-start(f16[2,64,256]{2,1,0:T(8,128)(2,1)S(1)} %get-tuple-element.83), channel_id=1, source_target_pairs={{0,6},{1,7},{2,4},{3,5},{4,2},{5,3},{6,0},{7,1},{8,14},{9,15},{10,... | collective-permute-start | bytes 196616 | tf_op jit(solution)/shard_map/ppermute | solution.py:147
  158.8 1.8 collective-permute-start.33
  161.2 2.1 %collective-permute-done.31 = f16[2,64,256]{2,1,0:T(8,128)(2,1)S(1)} collective-permute-done((f16[2,64,256]{2,1,0:T(8,128)(2,1)S(1)}, f16[2,64,256]{2,1,0:T(8,128)(2,1)S(1)}, u32[]{:S(2)}, u32[]{:S(2)}) %collective-permute-start.31) | collective-permute-done | bytes 65568 | tf_op jit(solution)/shard_map/ppermute | solution.py:147
  167.9 3.8 %collective-permute-start.37 = (f16[2,64,256]{2,1,0:T(8,128)(2,1)S(1)}, f16[2,64,256]{2,1,0:T(8,128)(2,1)S(1)}, u32[]{:S(2)}, u32[]{:S(2)}) collective-permute-start(f16[2,64,256]{2,1,0:T(8,128)(2,1)S(1)} %get-tuple-element.80), channel_id=1, source_target_pairs={{0,6},{1,7},{2,4},{3,5},{4,2},{5,3},{6,0},{7,1},{8,14},{9,15},{10,... | collective-permute-start | bytes 196616 | tf_op jit(solution)/shard_map/ppermute | solution.py:147
  174.7 2.7 %collective-permute-done.36 = f16[2,64,256]{2,1,0:T(8,128)(2,1)S(1)} collective-permute-done((f16[2,64,256]{2,1,0:T(8,128)(2,1)S(1)}, f16[2,64,256]{2,1,0:T(8,128)(2,1)S(1)}, u32[]{:S(2)}, u32[]{:S(2)}) %collective-permute-start.36) | collective-permute-done | bytes 65568 | tf_op jit(solution)/shard_map/ppermute | solution.py:147
  179.6 2.2 %collective-permute-start.43 = (f16[2,64,256]{2,1,0:T(8,128)(2,1)S(1)}, f16[2,64,256]{2,1,0:T(8,128)(2,1)S(1)}, u32[]{:S(2)}, u32[]{:S(2)}) collective-permute-start(f16[2,64,256]{2,1,0:T(8,128)(2,1)S(1)} %reshape.147), channel_id=1, source_target_pairs={{0,6},{1,7},{2,4},{3,5},{4,2},{5,3},{6,0},{7,1},{8,14},{9,15},{10,... | collective-permute-start | bytes 196616 | tf_op jit(solution)/shard_map/ppermute | solution.py:147
  186.2 2.5 %collective-permute-done.42 = f16[2,64,256]{2,1,0:T(8,128)(2,1)S(1)} collective-permute-done((f16[2,64,256]{2,1,0:T(8,128)(2,1)S(1)}, f16[2,64,256]{2,1,0:T(8,128)(2,1)S(1)}, u32[]{:S(2)}, u32[]{:S(2)}) %collective-permute-start.42) | collective-permute-done | bytes 65568 | tf_op jit(solution)/shard_map/ppermute | solution.py:147
  188.8 1.9 collective-permute-start.50
  190.6 2.6 %collective-permute-start.48 = (f16[2,64,256]{2,1,0:T(8,128)(2,1)S(1)}, f16[2,64,256]{2,1,0:T(8,128)(2,1)S(1)}, u32[]{:S(2)}, u32[]{:S(2)}) collective-permute-start(f16[2,64,256]{2,1,0:T(8,128)(2,1)S(1)} %reshape.151), channel_id=1, source_target_pairs={{0,2},{1,3},{2,0},{3,1},{4,6},{5,7},{6,4},{7,5},{8,10},{9,11},{10,... | collective-permute-start | bytes 196616 | tf_op jit(solution)/shard_map/ppermute | solution.py:147
  195.2 2.0 collective-permute-done.49
  197.9 2.7 %collective-permute-done.47 = f16[4,2,64,256]{3,2,1,0:T(8,128)(2,1)S(1)} collective-permute-done((f16[4,2,64,256]{3,2,1,0:T(8,128)(2,1)S(1)}, f16[4,2,64,256]{3,2,1,0:T(8,128)(2,1)S(1)}, u32[]{:S(2)}, u32[]{:S(2)}) %collective-permute-start.47) | collective-permute-done | bytes 262176 | tf_op jit(solution)/shard_map/ppermute | solution.py:147
  200.9 5.0 %collective-permute-done.51 = f16[4,2,64,256]{3,2,1,0:T(8,128)(2,1)S(1)} collective-permute-done((f16[4,2,64,256]{3,2,1,0:T(8,128)(2,1)S(1)}, f16[4,2,64,256]{3,2,1,0:T(8,128)(2,1)S(1)}, u32[]{:S(2)}, u32[]{:S(2)}) %collective-permute-start.51) | collective-permute-done | bytes 262176 | tf_op jit(solution)/shard_map/ppermute | solution.py:147
  (165 shorter events, 52.0 us)
Async XLA Ops:
  1.8 8.3 %collective-permute-start = (bf16[2,2,64,256]{3,2,1,0:T(8,128)(2,1)}, bf16[2,2,64,256]{3,2,1,0:T(8,128)(2,1)S(1)}, u32[]{:S(2)}, u32[]{:S(2)}) collective-permute-start(bf16[2,2,64,256]{3,2,1,0:T(8,128)(2,1)} %get-tuple-element.40), channel_id=1, source_target_pairs={{0,2},{1,3},{2,0},{3,1},{4,6},{5,7},{6,4},{7,5},{8,10},{9,11},{10,... | collective-permute-start | bytes 393224 | tf_op jit(solution)/shard_map/ppermute | solution.py:147
  4.8 13.2 %collective-permute-start.1 = (bf16[2,2,64,256]{3,2,1,0:T(8,128)(2,1)}, bf16[2,2,64,256]{3,2,1,0:T(8,128)(2,1)S(1)}, u32[]{:S(2)}, u32[]{:S(2)}) collective-permute-start(bf16[2,2,64,256]{3,2,1,0:T(8,128)(2,1)} %get-tuple-element.40), channel_id=1, source_target_pairs={{0,4},{1,5},{2,6},{3,7},{4,0},{5,1},{6,2},{7,3},{8,12},{9,13},{10,... | collective-permute-start | bytes 393224 | tf_op jit(solution)/shard_map/ppermute | solution.py:147
  7.4 10.6 %collective-permute-start.2 = (bf16[2,2,64,256]{3,2,1,0:T(8,128)(2,1)}, bf16[2,2,64,256]{3,2,1,0:T(8,128)(2,1)S(1)}, u32[]{:S(2)}, u32[]{:S(2)}) collective-permute-start(bf16[2,2,64,256]{3,2,1,0:T(8,128)(2,1)} %get-tuple-element.40), channel_id=1, source_target_pairs={{0,6},{1,7},{2,4},{3,5},{4,2},{5,3},{6,0},{7,1},{8,14},{9,15},{10,... | collective-permute-start | bytes 393224 | tf_op jit(solution)/shard_map/ppermute | solution.py:147
  18.0 9.5 %collective-permute-start.5 = (bf16[2,2,64,256]{3,2,1,0:T(8,128)(2,1)}, bf16[2,2,64,256]{3,2,1,0:T(8,128)(2,1)S(1)}, u32[]{:S(2)}, u32[]{:S(2)}) collective-permute-start(bf16[2,2,64,256]{3,2,1,0:T(8,128)(2,1)} %get-tuple-element.39), channel_id=1, source_target_pairs={{0,6},{1,7},{2,4},{3,5},{4,2},{5,3},{6,0},{7,1},{8,14},{9,15},{10,... | collective-permute-start | bytes 393224 | tf_op jit(solution)/shard_map/ppermute | solution.py:147
  20.2 14.5 %collective-permute-start.4 = (bf16[2,2,64,256]{3,2,1,0:T(8,128)(2,1)}, bf16[2,2,64,256]{3,2,1,0:T(8,128)(2,1)S(1)}, u32[]{:S(2)}, u32[]{:S(2)}) collective-permute-start(bf16[2,2,64,256]{3,2,1,0:T(8,128)(2,1)} %get-tuple-element.39), channel_id=1, source_target_pairs={{0,4},{1,5},{2,6},{3,7},{4,0},{5,1},{6,2},{7,3},{8,12},{9,13},{10,... | collective-permute-start | bytes 393224 | tf_op jit(solution)/shard_map/ppermute | solution.py:147
  21.4 13.4 %collective-permute-start.3 = (bf16[2,2,64,256]{3,2,1,0:T(8,128)(2,1)}, bf16[2,2,64,256]{3,2,1,0:T(8,128)(2,1)S(1)}, u32[]{:S(2)}, u32[]{:S(2)}) collective-permute-start(bf16[2,2,64,256]{3,2,1,0:T(8,128)(2,1)} %get-tuple-element.39), channel_id=1, source_target_pairs={{0,2},{1,3},{2,0},{3,1},{4,6},{5,7},{6,4},{7,5},{8,10},{9,11},{10,... | collective-permute-start | bytes 393224 | tf_op jit(solution)/shard_map/ppermute | solution.py:147
  25.8 8.8 %collective-permute-start.14 = (bf16[4,2,64,256]{3,2,1,0:T(8,128)(2,1)S(1)}, bf16[4,2,64,256]{3,2,1,0:T(8,128)(2,1)S(1)}, u32[]{:S(2)}, u32[]{:S(2)}) collective-permute-start(bf16[4,2,64,256]{3,2,1,0:T(8,128)(2,1)S(1)} %get-tuple-element.86), channel_id=1, source_target_pairs={{0,16},{1,17},{2,18},{3,19},{4,20},{5,21},{6,22},{7,23},{8,24},{9,... | collective-permute-start | bytes 786440 | tf_op jit(solution)/shard_map/ppermute | solution.py:147
  30.7 12.8 %collective-permute-start.12 = (bf16[2,4,2,64,256]{4,3,2,1,0:T(8,128)(2,1)S(1)}, bf16[2,4,2,64,256]{4,3,2,1,0:T(8,128)(2,1)S(1)}, u32[]{:S(2)}, u32[]{:S(2)}) collective-permute-start(bf16[2,4,2,64,256]{4,3,2,1,0:T(8,128)(2,1)S(1)} %pad_maximum_fusion.2.refs_0_), channel_id=1, source_target_pairs={{0,16},{1,17},{2,18},{3,19},{4,20},{5,21},{6,22},{7,23},{8,24},{9,... | collective-permute-start | bytes 1572872 | tf_op jit(solution)/shard_map/ppermute | solution.py:147
  34.7 10.7 %collective-permute-start.15 = (bf16[2,4,2,64,256]{4,3,2,1,0:T(8,128)(2,1)S(1)}, bf16[2,4,2,64,256]{4,3,2,1,0:T(8,128)(2,1)S(1)}, u32[]{:S(2)}, u32[]{:S(2)}) collective-permute-start(bf16[2,4,2,64,256]{4,3,2,1,0:T(8,128)(2,1)S(1)} %pad_maximum_fusion.3.refs_4_), channel_id=1, source_target_pairs={{0,1},{1,0},{2,3},{3,2},{4,5},{5,4},{6,7},{7,6},{8,9},{9,8},{10,11... | collective-permute-start | bytes 1572872 | tf_op jit(solution)/shard_map/ppermute | solution.py:147
  34.9 13.3 %collective-permute-start.6 = (bf16[4,2,64,256]{3,2,1,0:T(8,128)(2,1)S(1)}, bf16[4,2,64,256]{3,2,1,0:T(8,128)(2,1)S(1)}, u32[]{:S(2)}, u32[]{:S(2)}) collective-permute-start(bf16[4,2,64,256]{3,2,1,0:T(8,128)(2,1)S(1)} %get-tuple-element.92), channel_id=1, source_target_pairs={{0,1},{1,0},{2,3},{3,2},{4,5},{5,4},{6,7},{7,6},{8,9},{9,8},{10,11... | collective-permute-start | bytes 786440 | tf_op jit(solution)/shard_map/ppermute | solution.py:147
  37.0 21.6 %collective-permute-start.11 = (bf16[2,4,2,64,256]{4,3,2,1,0:T(8,128)(2,1)S(1)}, bf16[2,4,2,64,256]{4,3,2,1,0:T(8,128)(2,1)S(1)}, u32[]{:S(2)}, u32[]{:S(2)}) collective-permute-start(bf16[2,4,2,64,256]{4,3,2,1,0:T(8,128)(2,1)S(1)} %pad_maximum_fusion.2.refs_0_), channel_id=1, source_target_pairs={{0,8},{1,9},{2,10},{3,11},{4,12},{5,13},{6,14},{7,15},{8,0},{9,1},... | collective-permute-start | bytes 1572872 | tf_op jit(solution)/shard_map/ppermute | solution.py:147
  37.0 22.5 %collective-permute-start.16 = (bf16[2,4,2,64,256]{4,3,2,1,0:T(8,128)(2,1)S(1)}, bf16[2,4,2,64,256]{4,3,2,1,0:T(8,128)(2,1)S(1)}, u32[]{:S(2)}, u32[]{:S(2)}) collective-permute-start(bf16[2,4,2,64,256]{4,3,2,1,0:T(8,128)(2,1)S(1)} %pad_maximum_fusion.3.refs_4_), channel_id=1, source_target_pairs={{0,8},{1,9},{2,10},{3,11},{4,12},{5,13},{6,14},{7,15},{8,0},{9,1},... | collective-permute-start | bytes 1572872 | tf_op jit(solution)/shard_map/ppermute | solution.py:147
  43.5 16.0 %collective-permute-start.13 = (bf16[2,4,2,64,256]{4,3,2,1,0:T(8,128)(2,1)S(1)}, bf16[2,4,2,64,256]{4,3,2,1,0:T(8,128)(2,1)}, u32[]{:S(2)}, u32[]{:S(2)}) collective-permute-start(bf16[2,4,2,64,256]{4,3,2,1,0:T(8,128)(2,1)S(1)} %collective-permute-done.12.refs_2_), channel_id=1, source_target_pairs={{0,8},{1,9},{2,10},{3,11},{4,12},{5,13},{6,14},{7,15},{8,0},{9,1},... | collective-permute-start | bytes 1572872 | tf_op jit(solution)/shard_map/ppermute | solution.py:147
  45.4 14.1 %collective-permute-start.17 = (bf16[2,4,2,64,256]{4,3,2,1,0:T(8,128)(2,1)S(1)}, bf16[2,4,2,64,256]{4,3,2,1,0:T(8,128)(2,1)}, u32[]{:S(2)}, u32[]{:S(2)}) collective-permute-start(bf16[2,4,2,64,256]{4,3,2,1,0:T(8,128)(2,1)S(1)} %collective-permute-done.15.refs_5_), channel_id=1, source_target_pairs={{0,8},{1,9},{2,10},{3,11},{4,12},{5,13},{6,14},{7,15},{8,0},{9,1},... | collective-permute-start | bytes 1572872 | tf_op jit(solution)/shard_map/ppermute | solution.py:147
  48.9 7.1 %collective-permute-start.8 = (bf16[4,2,64,256]{3,2,1,0:T(8,128)(2,1)}, bf16[4,2,64,256]{3,2,1,0:T(8,128)(2,1)}, u32[]{:S(2)}, u32[]{:S(2)}) collective-permute-start(bf16[4,2,64,256]{3,2,1,0:T(8,128)(2,1)} %get-tuple-element.90), channel_id=1, source_target_pairs={{0,16},{1,17},{2,18},{3,19},{4,20},{5,21},{6,22},{7,23},{8,24},{9,... | collective-permute-start | bytes 786440 | tf_op jit(solution)/shard_map/ppermute | solution.py:147
  56.0 31.8 %collective-permute-start.7 = (bf16[2,4,2,64,256]{4,3,2,1,0:T(8,128)(2,1)S(1)}, bf16[2,4,2,64,256]{4,3,2,1,0:T(8,128)(2,1)S(1)}, u32[]{:S(2)}, u32[]{:S(2)}) collective-permute-start(bf16[2,4,2,64,256]{4,3,2,1,0:T(8,128)(2,1)S(1)} %pad_maximum_fusion.refs_0_), channel_id=1, source_target_pairs={{0,16},{1,17},{2,18},{3,19},{4,20},{5,21},{6,22},{7,23},{8,24},{9,... | collective-permute-start | bytes 1572872 | tf_op jit(solution)/shard_map/ppermute | solution.py:147
  58.6 29.2 %collective-permute-start.9 = (bf16[2,4,2,64,256]{4,3,2,1,0:T(8,128)(2,1)S(1)}, bf16[2,4,2,64,256]{4,3,2,1,0:T(8,128)(2,1)S(1)}, u32[]{:S(2)}, u32[]{:S(2)}) collective-permute-start(bf16[2,4,2,64,256]{4,3,2,1,0:T(8,128)(2,1)S(1)} %pad_maximum_fusion.1.refs_4_), channel_id=1, source_target_pairs={{0,1},{1,0},{2,3},{3,2},{4,5},{5,4},{6,7},{7,6},{8,9},{9,8},{10,11... | collective-permute-start | bytes 1572872 | tf_op jit(solution)/shard_map/ppermute | solution.py:147
  88.8 32.8 %collective-permute-start.18 = (f32[16,2,64,256]{3,2,1,0:T(8,128)}, f32[16,2,64,256]{3,2,1,0:T(8,128)}, u32[]{:S(2)}, u32[]{:S(2)}) collective-permute-start(f32[16,2,64,256]{3,2,1,0:T(8,128)} %get-tuple-element.47), channel_id=1, source_target_pairs={{0,8},{1,9},{2,10},{3,11},{4,12},{5,13},{6,14},{7,15},{8,0},{9,1},... | collective-permute-start | bytes 6291464 | tf_op jit(solution)/shard_map/ppermute | solution.py:147
  121.5 14.1 %collective-permute-start.25 = (f32[16,2,64,256]{3,2,1,0:T(8,128)}, f32[16,2,64,256]{3,2,1,0:T(8,128)}, u32[]{:S(2)}, u32[]{:S(2)}) collective-permute-start(f32[16,2,64,256]{3,2,1,0:T(8,128)} %get-tuple-element.53), channel_id=1, source_target_pairs={{0,8},{1,9},{2,10},{3,11},{4,12},{5,13},{6,14},{7,15},{8,0},{9,1},... | collective-permute-start | bytes 6291464 | tf_op jit(solution)/shard_map/ppermute | solution.py:147
  125.4 9.0 %collective-permute-start.19 = (f16[8,2,1,32,256]{4,3,2,1,0:T(8,128)(2,1)}, f16[8,2,1,32,256]{4,3,2,1,0:T(8,128)(2,1)}, u32[]{:S(2)}, u32[]{:S(2)}) collective-permute-start(f16[8,2,1,32,256]{4,3,2,1,0:T(8,128)(2,1)} %constant_dynamic-slice_fusion.17), channel_id=1, source_target_pairs={{0,16},{1,17},{2,18},{3,19},{4,20},{5,21},{6,22},{7,23},{8,24},{9,... | collective-permute-start | bytes 786440 | tf_op jit(solution)/shard_map/ppermute | solution.py:147
  125.6 9.9 %collective-permute-start.20 = (f16[4,2,2,32,256]{4,3,1,2,0:T(8,128)(2,1)S(1)}, f16[4,2,2,32,256]{4,3,1,2,0:T(8,128)(2,1)S(1)}, u32[]{:S(2)}, u32[]{:S(2)}) collective-permute-start(f16[4,2,2,32,256]{4,3,1,2,0:T(8,128)(2,1)S(1)} %bitcast.126), channel_id=1, source_target_pairs={{0,1},{1,0},{2,3},{3,2},{4,5},{5,4},{6,7},{7,6},{8,9},{9,8},{10,11... | collective-permute-start | bytes 786440 | tf_op jit(solution)/shard_map/ppermute | solution.py:147
  138.2 6.5 %collective-permute-start.27 = (f16[4,2,1,32,256]{4,3,1,2,0:T(8,128)(2,1)S(1)}, f16[4,2,1,32,256]{4,3,1,2,0:T(8,128)(2,1)S(1)}, u32[]{:S(2)}, u32[]{:S(2)}) collective-permute-start(f16[4,2,1,32,256]{4,3,1,2,0:T(8,128)(2,1)S(1)} %constant_dynamic-slice_fusion.14), channel_id=1, source_target_pairs={{0,16},{1,17},{2,18},{3,19},{4,20},{5,21},{6,22},{7,23},{8,24},{9,... | collective-permute-start | bytes 393224 | tf_op jit(solution)/shard_map/ppermute | solution.py:147
  139.1 9.8 %collective-permute-start.28 = (f16[8,2,1,32,256]{4,3,2,1,0:T(8,128)(2,1)S(1)}, f16[8,2,1,32,256]{4,3,2,1,0:T(8,128)(2,1)S(1)}, u32[]{:S(2)}, u32[]{:S(2)}) collective-permute-start(f16[8,2,1,32,256]{4,3,2,1,0:T(8,128)(2,1)S(1)} %constant_dynamic-slice_fusion.13), channel_id=1, source_target_pairs={{0,16},{1,17},{2,18},{3,19},{4,20},{5,21},{6,22},{7,23},{8,24},{9,... | collective-permute-start | bytes 786440 | tf_op jit(solution)/shard_map/ppermute | solution.py:147
  140.6 8.4 %collective-permute-start.29 = (f16[4,2,2,32,256]{4,3,1,2,0:T(8,128)(2,1)S(1)}, f16[4,2,2,32,256]{4,3,1,2,0:T(8,128)(2,1)S(1)}, u32[]{:S(2)}, u32[]{:S(2)}) collective-permute-start(f16[4,2,2,32,256]{4,3,1,2,0:T(8,128)(2,1)S(1)} %bitcast.127), channel_id=1, source_target_pairs={{0,1},{1,0},{2,3},{3,2},{4,5},{5,4},{6,7},{7,6},{8,9},{9,8},{10,11... | collective-permute-start | bytes 786440 | tf_op jit(solution)/shard_map/ppermute | solution.py:147
  149.3 11.9 %collective-permute-start.32 = (f16[2,64,256]{2,1,0:T(8,128)(2,1)S(1)}, f16[2,64,256]{2,1,0:T(8,128)(2,1)S(1)}, u32[]{:S(2)}, u32[]{:S(2)}) collective-permute-start(f16[2,64,256]{2,1,0:T(8,128)(2,1)S(1)} %get-tuple-element.83), channel_id=1, source_target_pairs={{0,6},{1,7},{2,4},{3,5},{4,2},{5,3},{6,0},{7,1},{8,14},{9,15},{10,... | collective-permute-start | bytes 196616 | tf_op jit(solution)/shard_map/ppermute | solution.py:147
  167.9 6.7 %collective-permute-start.37 = (f16[2,64,256]{2,1,0:T(8,128)(2,1)S(1)}, f16[2,64,256]{2,1,0:T(8,128)(2,1)S(1)}, u32[]{:S(2)}, u32[]{:S(2)}) collective-permute-start(f16[2,64,256]{2,1,0:T(8,128)(2,1)S(1)} %get-tuple-element.80), channel_id=1, source_target_pairs={{0,6},{1,7},{2,4},{3,5},{4,2},{5,3},{6,0},{7,1},{8,14},{9,15},{10,... | collective-permute-start | bytes 196616 | tf_op jit(solution)/shard_map/ppermute | solution.py:147
  179.6 6.6 %collective-permute-start.43 = (f16[2,64,256]{2,1,0:T(8,128)(2,1)S(1)}, f16[2,64,256]{2,1,0:T(8,128)(2,1)S(1)}, u32[]{:S(2)}, u32[]{:S(2)}) collective-permute-start(f16[2,64,256]{2,1,0:T(8,128)(2,1)S(1)} %reshape.147), channel_id=1, source_target_pairs={{0,6},{1,7},{2,4},{3,5},{4,2},{5,3},{6,0},{7,1},{8,14},{9,15},{10,... | collective-permute-start | bytes 196616 | tf_op jit(solution)/shard_map/ppermute | solution.py:147
  181.8 6.8 %collective-permute-start.42 = (f16[2,64,256]{2,1,0:T(8,128)(2,1)S(1)}, f16[2,64,256]{2,1,0:T(8,128)(2,1)S(1)}, u32[]{:S(2)}, u32[]{:S(2)}) collective-permute-start(f16[2,64,256]{2,1,0:T(8,128)(2,1)S(1)} %reshape.147), channel_id=1, source_target_pairs={{0,4},{1,5},{2,6},{3,7},{4,0},{5,1},{6,2},{7,3},{8,12},{9,13},{10,... | collective-permute-start | bytes 196616 | tf_op jit(solution)/shard_map/ppermute | solution.py:147
  190.6 6.5 %collective-permute-start.49 = (f16[2,64,256]{2,1,0:T(8,128)(2,1)S(1)}, f16[2,64,256]{2,1,0:T(8,128)(2,1)S(1)}, u32[]{:S(2)}, u32[]{:S(2)}) collective-permute-start(f16[2,64,256]{2,1,0:T(8,128)(2,1)S(1)} %reshape.151), channel_id=1, source_target_pairs={{0,4},{1,5},{2,6},{3,7},{4,0},{5,1},{6,2},{7,3},{8,12},{9,13},{10,... | collective-permute-start | bytes 196616 | tf_op jit(solution)/shard_map/ppermute | solution.py:147
  190.6 6.5 %collective-permute-start.48 = (f16[2,64,256]{2,1,0:T(8,128)(2,1)S(1)}, f16[2,64,256]{2,1,0:T(8,128)(2,1)S(1)}, u32[]{:S(2)}, u32[]{:S(2)}) collective-permute-start(f16[2,64,256]{2,1,0:T(8,128)(2,1)S(1)} %reshape.151), channel_id=1, source_target_pairs={{0,2},{1,3},{2,0},{3,1},{4,6},{5,7},{6,4},{7,5},{8,10},{9,11},{10,... | collective-permute-start | bytes 196616 | tf_op jit(solution)/shard_map/ppermute | solution.py:147
  193.2 7.4 %collective-permute-start.47 = (f16[4,2,64,256]{3,2,1,0:T(8,128)(2,1)S(1)}, f16[4,2,64,256]{3,2,1,0:T(8,128)(2,1)S(1)}, u32[]{:S(2)}, u32[]{:S(2)}) collective-permute-start(f16[4,2,64,256]{3,2,1,0:T(8,128)(2,1)S(1)} %pad_maximum_fusion.8), channel_id=1, source_target_pairs={{0,1},{1,0},{2,3},{3,2},{4,5},{5,4},{6,7},{7,6},{8,9},{9,8},{10,11... | collective-permute-start | bytes 786440 | tf_op jit(solution)/shard_map/ppermute | solution.py:147
  197.3 8.7 %collective-permute-start.51 = (f16[4,2,64,256]{3,2,1,0:T(8,128)(2,1)S(1)}, f16[4,2,64,256]{3,2,1,0:T(8,128)(2,1)S(1)}, u32[]{:S(2)}, u32[]{:S(2)}) collective-permute-start(f16[4,2,64,256]{3,2,1,0:T(8,128)(2,1)S(1)} %get-tuple-element.78), channel_id=1, source_target_pairs={{0,1},{1,0},{2,3},{3,2},{4,5},{5,4},{6,7},{7,6},{8,9},{9,8},{10,11... | collective-permute-start | bytes 786440 | tf_op jit(solution)/shard_map/ppermute | solution.py:147
  (29 other events, 216.9 us)
